TPU v7x, 32 devices: a whole 2x2x4 slice. The times are simulated.
32 devices in a mesh: dp: 8 (over z, x), tensor: 4 (over y, core).
Axes of the slice: x: 2, y: 2, z: 4, core: 2. Of those that a mesh axis runs over, the one named last changes fastest.
Arguments:
- layer_input: bfloat16 [8192, 2048], P(('dp', 'tensor')), may hold values from -6 to 6
- query_weight: bfloat16 [2048, 2048], P('dp', 'tensor'), may hold values from -0.125 to 0.125
- key_weight: bfloat16 [2048, 2048], P('dp', 'tensor'), may hold values from -0.125 to 0.125
- value_weight: bfloat16 [2048, 2048], P('dp', 'tensor'), may hold values from -0.125 to 0.125
- out_weight: bfloat16 [2048, 2048], P('dp', 'tensor'), may hold values from -2 to 2
- gate_weight: bfloat16 [2048, 8192], P('dp', 'tensor'), may hold values from -0.125 to 0.125
- up_weight: bfloat16 [2048, 8192], P('dp', 'tensor'), may hold values from -0.125 to 0.125
- down_weight: bfloat16 [2048, 8192], P('dp', 'tensor'), may hold values from -0.0625 to 0.0625
- attention_gain: bfloat16 [2048], P('dp'), may hold values from 0.25 to 1.75
- feed_gain: bfloat16 [2048], P('dp'), may hold values from 0.25 to 1.75
- out_cotangent: bfloat16 [8192, 2048], P(('dp', 'tensor')), may hold values from -6 to 6
Outputs:
- layer_output: float32 [8192, 2048], P(('dp', 'tensor'))
- input_grad: float32 [8192, 2048], P(('dp', 'tensor'))
- query_grad: float32 [2048, 2048], P('dp', 'tensor')
- key_grad: float32 [2048, 2048], P('dp', 'tensor')
- value_grad: float32 [2048, 2048], P('dp', 'tensor')
- out_grad: float32 [2048, 2048], P('dp', 'tensor')
- gate_grad: float32 [2048, 8192], P('dp', 'tensor')
- up_grad: float32 [2048, 8192], P('dp', 'tensor')
- down_grad: float32 [2048, 8192], P('dp', 'tensor')
- attention_gain_grad: float32 [2048], P(('dp', 'tensor'))
- feed_gain_grad: float32 [2048], P(('dp', 'tensor'))
All inputs are finite; a program needn't handle non-finite values.
Results may differ from a plain program's by a relative error of at most 0.019.
Values may be sent and summed in bfloat16 or wider, within the bound.
A program may use at most 256 MiB of HBM per device.

v0:
```python
import jax
import jax.numpy as jnp
from jax import lax
from jax.experimental import pallas as pl
from jax.experimental.pallas import tpu as pltpu
from jax.sharding import Mesh, PartitionSpec as P

HD = 64
LEN = 1024
BLK = 256
PAIR = 2 * HD
CHUNKS = 2

epsilon = 1e-05
rope_base = 130000.0
group = ("i", "y", "c")
swap = [(0, 1), (1, 0)]


def contract(left_side, right_side, left_dim, right_dim):
    return lax.dot_general(
        left_side,
        right_side,
        (((left_dim,), (right_dim,)), ((), ())),
        preferred_element_type=jnp.float32,
    )


MESH = pl.DeviceIdType.MESH


def row_partner(shift, outer):
    return {"o": lax.rem(lax.axis_index("o") + shift, outer)}


def greet_partners(outer=1):
    barrier = pltpu.get_barrier_semaphore()
    partners = [{axis: 1 - lax.axis_index(axis)} for axis in group]
    partners += [row_partner(shift, outer) for shift in range(1, outer)]
    for partner in partners:
        pl.semaphore_signal(barrier, inc=1, device_id=partner, device_id_type=MESH)
    pl.semaphore_wait(barrier, len(partners))


def send_along(axis, source, target, semaphores, slot):
    return pltpu.make_async_remote_copy(
        src_ref=source,
        dst_ref=target,
        send_sem=semaphores.at[0, slot],
        recv_sem=semaphores.at[1, slot],
        device_id={axis: 1 - lax.axis_index(axis)},
        device_id_type=MESH,
    )


def first_row(flips, rows):
    i, y, c = [
        1 - lax.axis_index(axis) if axis in flips else lax.axis_index(axis) for axis in group
    ]
    return pl.multiple_of(((i * 2 + y) * 2 + c) * rows, rows)


def gather_kernel(outer, *refs):
    source, target, semaphores, own_semaphore = refs
    rows = source.shape[0]
    half = rows // 2
    greet_partners(outer)

    def place(flips, part=None):
        start = first_row(flips, rows)
        if part is None:
            return target.at[pl.ds(start, rows), :]
        return target.at[pl.ds(start + part * half, half), :]

    started = []

    def send(axis, source, target, slot):
        copy = send_along(axis, source, target, semaphores, slot)
        copy.start()
        started.append(copy)
        return copy

    own = pltpu.make_async_copy(source, place(()), own_semaphore)
    own.start()
    top, bottom = source.at[pl.ds(0, half), :], source.at[pl.ds(half, half), :]
    i_top = send("i", top, place((), 0), 0)
    y_bottom = send("y", bottom, place((), 1), 1)
    i_bottom = send("i", bottom, place((), 1), 2)
    y_top = send("y", top, place((), 0), 3)
    core = [send("c", source, place(()), 4)]
    i_top.wait_recv()
    across_top = send("y", place(("i",), 0), place(("i",), 0), 5)
    y_bottom.wait_recv()
    across_bottom = send("i", place(("y",), 1), place(("y",), 1), 6)
    i_bottom.wait_recv()
    core.append(send("c", place(("i",)), place(("i",)), 7))
    y_top.wait_recv()
    core.append(send("c", place(("y",)), place(("y",)), 8))
    across_top.wait_recv()
    core.append(send("c", place(("i", "y"), 0), place(("i", "y"), 0), 9))
    across_bottom.wait_recv()
    core.append(send("c", place(("i", "y"), 1), place(("i", "y"), 1), 10))
    for copy in core:
        copy.wait_recv()
    own.wait()
    for copy in started:
        copy.wait_send()


def opening_kernel(outer, token_ref, gain_ref, token_out, gain_out, *scratch):
    semaphores, own_semaphore, side_semaphores, row_semaphores = scratch
    me, side = lax.axis_index("o"), lax.axis_index("i")

    gather_kernel(outer, token_ref, token_out, semaphores, own_semaphore)
    gain_out[me * 2 + side] = gain_ref[...]
    along = send_along("i", gain_ref, gain_out.at[me * 2 + side], side_semaphores, 0)
    along.start()
    started = [along]

    def send_rows(source, slot, first):
        for shift in range(1, outer):
            copy = pltpu.make_async_remote_copy(
                src_ref=source,
                dst_ref=gain_out.at[slot],
                send_sem=row_semaphores.at[0, first, shift],
                recv_sem=row_semaphores.at[1, first, shift],
                device_id=row_partner(shift, outer),
                device_id_type=MESH,
            )
            copy.start()
            started.append(copy)

    send_rows(gain_ref, me * 2 + side, 0)
    along.wait_recv()
    send_rows(gain_out.at[me * 2 + 1 - side], me * 2 + 1 - side, 1)
    for copy in started[1:]:
        copy.wait_recv()
    for copy in started:
        copy.wait_send()


def opening_gather(array, gains, outer):
    rows, width = array.shape
    padded = jnp.pad(gains, ((0, 16 - gains.shape[0]), (0, 0)))
    vmem, hbm = pl.BlockSpec(memory_space=pltpu.VMEM), pl.BlockSpec(memory_space=pl.ANY)
    gathered, gain_rows = pl.pallas_call(
        lambda *refs: opening_kernel(outer, *refs),
        in_specs=[vmem] * 2,
        out_specs=[hbm, vmem],
        out_shape=[
            jax.ShapeDtypeStruct((8 * rows, width), array.dtype),
            jax.ShapeDtypeStruct((2 * outer, *padded.shape), gains.dtype),
        ],
        scratch_shapes=[
            pltpu.SemaphoreType.DMA((2, 11)),
            pltpu.SemaphoreType.DMA(()),
            pltpu.SemaphoreType.DMA((2, 1)),
            pltpu.SemaphoreType.DMA((2, 2, max(outer, 2))),
        ],
        compiler_params=pltpu.CompilerParams(collective_id=2, has_side_effects=True),
        cost_estimate=pl.CostEstimate(
            flops=0, bytes_accessed=200 * rows * width, transcendentals=0
        ),
        name="opening_gather",
    )(array, padded)
    return gathered, [gain_rows[:, which].reshape(-1) for which in range(2)]


def token_gather(array):
    rows, width = array.shape
    return pl.pallas_call(
        lambda *refs: gather_kernel(1, *refs),
        in_specs=[pl.BlockSpec(memory_space=pltpu.VMEM)],
        out_specs=pl.BlockSpec(memory_space=pl.ANY),
        out_shape=jax.ShapeDtypeStruct((8 * rows, width), array.dtype),
        scratch_shapes=[pltpu.SemaphoreType.DMA((2, 11)), pltpu.SemaphoreType.DMA(())],
        compiler_params=pltpu.CompilerParams(collective_id=1, has_side_effects=True),
        cost_estimate=pl.CostEstimate(
            flops=0, bytes_accessed=200 * rows * width, transcendentals=0
        ),
        name="token_gather",
    )(array)


def total_kernel(outer, part_ref, total_ref, held, stages, semaphores, row_semaphores):
    greet_partners(outer)
    started = []
    source, value = part_ref, part_ref[...]
    for step, axis in enumerate(group):
        copy = send_along(axis, source, held.at[step], semaphores, step)
        copy.start()
        started.append(copy)
        copy.wait_recv()
        value = value + held[step]
        stages[step] = value
        source = stages.at[step]
    copies = []
    for shift in range(1, outer):
        copy = pltpu.make_async_remote_copy(
            src_ref=source,
            dst_ref=held.at[2 + shift],
            send_sem=row_semaphores.at[0, shift],
            recv_sem=row_semaphores.at[1, shift],
            device_id=row_partner(shift, outer),
            device_id_type=MESH,
        )
        copy.start()
        copies.append(copy)
    for shift, copy in enumerate(copies):
        copy.wait_recv()
        value = value + held[3 + shift]
    total_ref[...] = value
    for copy in started + copies:
        copy.wait_send()


def sum_everywhere(part, outer):
    folded = part.reshape(-1, 128)
    spec = pl.BlockSpec(memory_space=pltpu.VMEM)
    return pl.pallas_call(
        lambda *refs: total_kernel(outer, *refs),
        in_specs=[spec],
        out_specs=spec,
        out_shape=jax.ShapeDtypeStruct(folded.shape, jnp.float32),
        scratch_shapes=[
            pltpu.VMEM((2 + outer, *folded.shape), jnp.float32),
            pltpu.VMEM((3, *folded.shape), jnp.float32),
            pltpu.SemaphoreType.DMA((2, 3)),
            pltpu.SemaphoreType.DMA((2, max(outer, 2))),
        ],
        compiler_params=pltpu.CompilerParams(collective_id=7, has_side_effects=True),
        name="sum_everywhere",
    )(folded).reshape(part.shape)


def scatter_kernel(windows, *refs):
    count = len(windows)
    lefts, rights, total = refs[:count], refs[count : 2 * count], refs[2 * count]
    (
        left_held,
        right_held,
        core_out,
        core_in,
        sums,
        first_i,
        first_y,
        second_i,
        second_y,
        left_semaphores,
        right_semaphores,
        semaphores,
    ) = refs[2 * count + 1 :]
    rows, width = total.shape
    half = rows // 2
    tile = 512
    relations = (("i", "y"), ("i",), ("y",), ())
    order = [(r, mine) for r in range(4) for mine in (False, True)]

    loads = []
    edge = 0
    for which, (left_start, right_start, depth) in enumerate(windows):
        copy = pltpu.make_async_copy(
            rights[which].at[:, pl.ds(right_start, depth)],
            right_held.at[:, pl.ds(edge, depth)],
            right_semaphores.at[which],
        )
        copy.start()
        loads.append(copy)
        edge += depth
    left_loads = []
    for step, (r, mine) in enumerate(order):
        flips = relations[r] if mine else relations[r] + ("c",)
        start = first_row(flips, rows)
        edge = 0
        row = []
        for which, (left_start, right_start, depth) in enumerate(windows):
            copy = pltpu.make_async_copy(
                lefts[which].at[pl.ds(start, rows), pl.ds(left_start, depth)],
                left_held.at[step, :, pl.ds(edge, depth)],
                left_semaphores.at[step, which],
            )
            copy.start()
            row.append(copy)
            edge += depth
        left_loads.append(row)
    greet_partners()
    for copy in loads:
        copy.wait()

    top, bottom = pl.ds(0, half), pl.ds(half, half)
    started = []

    def send(axis, source, target, slot):
        copy = send_along(axis, source, target, semaphores, slot)
        copy.start()
        started.append(copy)
        return copy

    core_copies, copies = [], {}
    for step, (r, mine) in enumerate(order):
        for copy in left_loads[step]:
            copy.wait()
        if mine:
            core_copies[r].wait_recv()

        def one_tile(t, carry):
            columns = pl.ds(pl.multiple_of(t * tile, tile), tile)
            part = contract(left_held[step], right_held[columns, :], 1, 1)
            if not mine:
                core_out[r, :, columns] = part.astype(jnp.bfloat16)
            elif r < 3:
                sums[r, :, columns] = (part + core_in[r, :, columns].astype(jnp.float32)).astype(
                    jnp.bfloat16
                )
            else:
                total[:, columns] = part + core_in[r, :, columns].astype(jnp.float32)
            return carry

        lax.fori_loop(0, width // tile, one_tile, 0)
        if not mine:
            core_copies.append(send("c", core_out.at[r], core_in.at[r], r))
        elif r == 0:
            copies["i1"] = send("i", sums.at[0, top, :], first_i.at[1], 4)
            copies["y1"] = send("y", sums.at[0, bottom, :], first_y.at[1], 5)
        elif r == 1:
            copies["i0"] = send("i", sums.at[1, top, :], first_i.at[0], 6)
        elif r == 2:
            copies["y0"] = send("y", sums.at[2, bottom, :], first_y.at[0], 7)
            copies["y1"].wait_recv()
            sums[1, bottom, :] = (
                sums[1, bottom, :].astype(jnp.float32) + first_y[1].astype(jnp.float32)
            ).astype(jnp.bfloat16)
            copies["i2"] = send("i", sums.at[1, bottom, :], second_i, 8)
            copies["i1"].wait_recv()
            sums[2, top, :] = (
                sums[2, top, :].astype(jnp.float32) + first_i[1].astype(jnp.float32)
            ).astype(jnp.bfloat16)
            copies["y2"] = send("y", sums.at[2, top, :], second_y, 9)
    copies["i0"].wait_recv()
    total[top, :] += first_i[0].astype(jnp.float32)
    copies["y0"].wait_recv()
    total[bottom, :] += first_y[0].astype(jnp.float32)
    copies["y2"].wait_recv()
    total[top, :] += second_y[...].astype(jnp.float32)
    copies["i2"].wait_recv()
    total[bottom, :] += second_i[...].astype(jnp.float32)
    for copy in started:
        copy.wait_send()


def product_sum(terms, number):
    rows, width = terms[0][0].shape[0] // 8, terms[0][2].shape[0]
    half = rows // 2
    count = len(terms)
    depth = sum(term[4] for term in terms)
    windows = [(term[1], term[3], term[4]) for term in terms]
    return pl.pallas_call(
        lambda *refs: scatter_kernel(windows, *refs),
        in_specs=[pl.BlockSpec(memory_space=pl.ANY)] * (2 * count),
        out_specs=pl.BlockSpec(memory_space=pltpu.VMEM),
        out_shape=jax.ShapeDtypeStruct((rows, width), jnp.float32),
        scratch_shapes=[
            pltpu.VMEM((8, rows, depth), jnp.bfloat16),
            pltpu.VMEM((width, depth), jnp.bfloat16),
            pltpu.VMEM((4, rows, width), jnp.bfloat16),
            pltpu.VMEM((4, rows, width), jnp.bfloat16),
            pltpu.VMEM((3, rows, width), jnp.bfloat16),
            pltpu.VMEM((2, half, width), jnp.bfloat16),
            pltpu.VMEM((2, half, width), jnp.bfloat16),
            pltpu.VMEM((half, width), jnp.bfloat16),
            pltpu.VMEM((half, width), jnp.bfloat16),
            pltpu.SemaphoreType.DMA((8, count)),
            pltpu.SemaphoreType.DMA((count,)),
            pltpu.SemaphoreType.DMA((2, 10)),
        ],
        compiler_params=pltpu.CompilerParams(collective_id=number, has_side_effects=True),
        cost_estimate=pl.CostEstimate(
            flops=16 * rows * depth * width, bytes_accessed=100 * rows * width, transcendentals=0
        ),
    )(*[term[0] for term in terms], *[term[2] for term in terms])


def rope_tables():
    half_dim = HD // 2
    lanes = jnp.arange(PAIR)
    inverse = rope_base ** (-((lanes % half_dim).astype(jnp.float32) * 2.0 / HD))
    angles = jnp.arange(LEN, dtype=jnp.float32)[:, None] * inverse[None, :]
    sign = jnp.where(lanes % HD < half_dim, -1.0, 1.0)
    return jnp.cos(angles), jnp.sin(angles) * sign[None, :]


def turn(values, cosine, signed_sine):
    half_dim = HD // 2
    lanes = lax.broadcasted_iota(jnp.int32, values.shape, 1)
    other = jnp.where(
        lanes % HD < half_dim,
        pltpu.roll(values, PAIR - half_dim, 1),
        pltpu.roll(values, half_dim, 1),
    )
    return values * cosine + other * signed_sine


def head_parts(values):
    lanes = lax.broadcasted_iota(jnp.int32, values.shape, 1)
    empty = jnp.zeros_like(values)
    return [jnp.where(lanes // HD == head, values, empty) for head in range(2)]


def forward_kernel(
    query_ref, key_ref, value_ref, cos_ref, sin_ref, q_out, k_out, v_out, attended_out
):
    cosine, sine = cos_ref[...], sin_ref[...]
    queries = turn(query_ref[...], cosine, sine).astype(jnp.bfloat16)
    keys = turn(key_ref[...], cosine, sine).astype(jnp.bfloat16)
    values = value_ref[...].astype(jnp.bfloat16)
    q_out[...] = queries
    k_out[...] = keys
    v_out[...] = values
    value_parts = head_parts(values)
    scaling = HD**-0.5
    for block in range(LEN // BLK):
        rows = slice(block * BLK, (block + 1) * BLK)
        seen = (block + 1) * BLK
        total = None
        for head, query_part in enumerate(head_parts(queries[rows])):
            scores = contract(query_part, keys[:seen], 1, 1) * scaling
            top = jnp.max(scores, axis=-1, keepdims=True)
            powers = jnp.exp(scores - top)
            weights = powers / jnp.sum(powers, axis=-1, keepdims=True)
            term = contract(weights.astype(jnp.bfloat16), value_parts[head][:seen], 1, 0)
            total = term if total is None else total + term
        attended_out[rows, :] = total.astype(jnp.bfloat16)


def backward_kernel(
    query_ref, key_ref, value_ref, grad_ref, cos_ref, sin_ref, q_out, k_out, v_out, key_acc, value_acc
):
    keys, values = key_ref[...], value_ref[...]
    key_parts = head_parts(keys)
    scaling = HD**-0.5
    key_acc[...] = jnp.zeros_like(key_acc)
    value_acc[...] = jnp.zeros_like(value_acc)
    for block in range(LEN // BLK):
        rows = slice(block * BLK, (block + 1) * BLK)
        seen = (block + 1) * BLK
        query_parts = head_parts(query_ref[rows, :])
        grad_parts = head_parts(grad_ref[rows, :])
        query_delta = None
        for head in range(2):
            scores = contract(query_parts[head], keys[:seen], 1, 1) * scaling
            top = jnp.max(scores, axis=-1, keepdims=True)
            powers = jnp.exp(scores - top)
            weights = powers / jnp.sum(powers, axis=-1, keepdims=True)
            grad_probs = contract(grad_parts[head], values[:seen], 1, 1)
            row_dot = jnp.sum(weights * grad_probs, axis=-1, keepdims=True)
            grad_scores = (weights * (grad_probs - row_dot) * scaling).astype(jnp.bfloat16)
            term = contract(grad_scores, key_parts[head][:seen], 1, 0)
            query_delta = term if query_delta is None else query_delta + term
            key_acc[:seen, :] += contract(grad_scores, query_parts[head], 0, 0)
            value_acc[:seen, :] += contract(weights.astype(jnp.bfloat16), grad_parts[head], 0, 0)
        q_out[rows, :] = turn(query_delta, cos_ref[rows, :], -sin_ref[rows, :]).astype(jnp.bfloat16)
    k_out[...] = turn(key_acc[...], cos_ref[...], -sin_ref[...]).astype(jnp.bfloat16)
    v_out[...] = value_acc[...].astype(jnp.bfloat16)


def attention_cost(rows, width, products):
    return pl.CostEstimate(
        flops=2 * products * rows * LEN * width,
        bytes_accessed=8 * rows * width * 2,
        transcendentals=rows * LEN * width // HD,
    )


def attention_forward(mixed, tables):
    rows, width = mixed.shape[0], mixed.shape[1] // 3
    pairs = width // PAIR

    def part(which):
        return pl.BlockSpec((LEN, PAIR), lambda s, p: (s, which * pairs + p))

    whole = pl.BlockSpec((LEN, PAIR), lambda s, p: (0, 0))
    return pl.pallas_call(
        forward_kernel,
        grid=(rows // LEN, pairs),
        in_specs=[part(0), part(1), part(2), whole, whole],
        out_specs=[part(0)] * 4,
        out_shape=[jax.ShapeDtypeStruct((rows, width), jnp.bfloat16)] * 4,
        cost_estimate=attention_cost(rows, width, 2),
        name="attention_forward",
    )(mixed, mixed, mixed, *tables)


def attention_backward(queries, keys, values, grads, tables):
    rows, width = queries.shape
    part = pl.BlockSpec((LEN, PAIR), lambda s, p: (s, p))
    whole = pl.BlockSpec((LEN, PAIR), lambda s, p: (0, 0))
    return pl.pallas_call(
        backward_kernel,
        grid=(rows // LEN, width // PAIR),
        in_specs=[part] * 4 + [whole] * 2,
        out_specs=[part] * 3,
        out_shape=[jax.ShapeDtypeStruct((rows, width), jnp.bfloat16)] * 3,
        scratch_shapes=[pltpu.VMEM((LEN, PAIR), jnp.float32)] * 2,
        cost_estimate=attention_cost(rows, width, 5),
        name="attention_backward",
    )(queries, keys, values, grads, *tables)


def feed_kernel(normed_ref, cotangent_ref, weight_ref, out_ref):
    chunk = out_ref.shape[1] // 3
    gate, up, down = [slice(which * chunk, (which + 1) * chunk) for which in range(3)]
    gate_pre = contract(normed_ref[...], weight_ref[:, gate], 1, 0)
    up_proj = contract(normed_ref[...], weight_ref[:, up], 1, 0)
    grad_act = contract(cotangent_ref[...], weight_ref[:, down], 1, 0)
    sigmoid_gate = jax.nn.sigmoid(gate_pre)
    silu_gate = gate_pre * sigmoid_gate
    gate_slope = sigmoid_gate * (1.0 + gate_pre * (1.0 - sigmoid_gate))
    out_ref[:, gate] = (grad_act * up_proj * gate_slope).astype(jnp.bfloat16)
    out_ref[:, up] = (grad_act * silu_gate).astype(jnp.bfloat16)
    out_ref[:, down] = (silu_gate * up_proj).astype(jnp.bfloat16)


def feed_units(normed, cotangents, weights):
    (rows, width), columns = normed.shape, weights.shape[1]
    tile = 256
    tokens = pl.BlockSpec((tile, width), lambda t: (t, 0))
    return pl.pallas_call(
        feed_kernel,
        grid=(rows // tile,),
        in_specs=[tokens, tokens, pl.BlockSpec((width, columns), lambda t: (0, 0))],
        out_specs=pl.BlockSpec((tile, columns), lambda t: (t, 0)),
        out_shape=jax.ShapeDtypeStruct((rows, columns), jnp.bfloat16),
        cost_estimate=pl.CostEstimate(
            flops=2 * rows * width * columns,
            bytes_accessed=2 * (2 * rows * width + width * columns + rows * columns),
            transcendentals=rows * columns // 3,
        ),
        name="feed_units",
    )(normed, cotangents, weights)


def weight_grads(terms):
    rows, width = terms[0][0].shape
    tile = 256
    operands, specs, plan = [], [], []
    for left, rights in terms:
        operands.append(left)
        specs.append(pl.BlockSpec((rows, tile), lambda t: (0, t)))
        for right, start, columns in rights:
            operands.append(right)
            specs.append(
                pl.BlockSpec((rows, columns), lambda t, block=start // columns: (0, block))
            )
        plan.append([columns for _, _, columns in rights])
    total = sum(sum(widths) for widths in plan)

    def kernel(*refs):
        edge, at = 0, 0
        for widths in plan:
            left = refs[at][...]
            at += 1
            for columns in widths:
                refs[-1][:, edge : edge + columns] = contract(left, refs[at][...], 0, 0).astype(
                    jnp.bfloat16
                )
                edge += columns
                at += 1

    return pl.pallas_call(
        kernel,
        grid=(width // tile,),
        in_specs=specs,
        out_specs=pl.BlockSpec((tile, total), lambda t: (t, 0)),
        out_shape=jax.ShapeDtypeStruct((width, total), jnp.bfloat16),
        cost_estimate=pl.CostEstimate(
            flops=2 * rows * width * total,
            bytes_accessed=2 * (2 * rows * width + width * total + rows * total),
            transcendentals=0,
        ),
    )(*operands)


def exchange_rows(weights, first, width):
    side = lax.axis_index("i")

    def columns(half):
        start = [half * (w.shape[1] // 2) + first for w in weights]
        return jnp.concatenate([w[:, a : a + width] for w, a in zip(weights, start)], axis=1)

    low, high = columns(0), columns(1)
    kept = jnp.where(side == 0, low, high)
    other = lax.ppermute(jnp.where(side == 0, high, low), "i", swap)
    return jnp.concatenate(
        [jnp.where(side == 0, kept, other), jnp.where(side == 0, other, kept)]
    )


def row_gather(values):
    return lax.all_gather(values, "o", axis=0, tiled=True)


def row_sum(partial_value):
    return lax.psum_scatter(partial_value, "o", scatter_dimension=0, tiled=True)


def exchange_columns(summed):
    side = lax.axis_index("i")
    rows = summed.shape[0] // 2
    kept = lax.dynamic_slice_in_dim(summed, side * rows, rows, axis=0)
    other = lax.ppermute(
        lax.dynamic_slice_in_dim(summed, (1 - side) * rows, rows, axis=0), "i", swap
    )
    return jnp.where(side == 0, kept, other), jnp.where(side == 0, other, kept)


def inverse_rms(values):
    return lax.rsqrt(jnp.mean(values * values, axis=-1, keepdims=True) + epsilon)


def per_device(
    layer_input,
    query_weight,
    key_weight,
    value_weight,
    out_weight,
    gate_weight,
    up_weight,
    down_weight,
    attention_gain,
    feed_gain,
    out_cotangent,
):
    head_width = query_weight.shape[1] // 2
    hidden = gate_weight.shape[1] // 2
    chunk = hidden // CHUNKS
    tables = rope_tables()
    outer = lax.axis_size("o")

    attention_rows = exchange_rows(
        (query_weight, key_weight, value_weight, out_weight), 0, head_width
    )
    attention_full = row_gather(attention_rows)
    feed_full = []
    for k in range(CHUNKS):
        feed_rows = exchange_rows((gate_weight, up_weight, down_weight), k * chunk, chunk)
        feed_full.append(row_gather(feed_rows))
    inputs_all, gains = opening_gather(layer_input, jnp.stack([attention_gain, feed_gain]), outer)
    inputs_all, late = lax.optimization_barrier((inputs_all, out_cotangent))
    cotangents = token_gather(late)
    gain_one, gain_two = [g.astype(jnp.float32) for g in gains]
    inputs_all = inputs_all.astype(jnp.float32)
    normed = (inputs_all * inverse_rms(inputs_all) * gain_one).astype(jnp.bfloat16)
    inputs = layer_input.astype(jnp.float32)
    inv_one = inverse_rms(inputs)
    normed_one = inputs * inv_one

    mixed = contract(normed, attention_full[:, : 3 * head_width], 1, 0)
    queries, keys, values, attended = attention_forward(mixed, tables)
    out_full = attention_full[:, 3 * head_width :]
    hidden_state = inputs + product_sum(
        [(attended, 0, attention_full, 3 * head_width, head_width)], 3
    )
    inv_two = inverse_rms(hidden_state)
    normed_two_raw = hidden_state * inv_two
    normed_two = token_gather((normed_two_raw * gain_two).astype(jnp.bfloat16))

    output_terms, grad_terms, feed_grads = [], [], []
    for k in range(CHUNKS):
        units = feed_units(normed_two, cotangents, feed_full[k])
        grads = weight_grads(
            [
                (normed_two, [(units, 0, 2 * chunk)]),
                (cotangents, [(units, 2 * chunk, chunk)]),
            ],
        )
        units, grads, normed_two, cotangents = lax.optimization_barrier(
            (units, grads, normed_two, cotangents)
        )
        summed = row_sum(grads)
        feed_grads.append(exchange_columns(summed))
        grad_terms.append((units, 0, feed_full[k], 0, 2 * chunk))
        output_terms.append((units, 2 * chunk, feed_full[k], 2 * chunk, chunk))

    grad_normed_two = product_sum(grad_terms, 4)
    feed_gain_part = jnp.sum(grad_normed_two * normed_two_raw, axis=0)
    scaled_two = grad_normed_two * gain_two
    grad_hidden = out_cotangent.astype(jnp.float32) + inv_two * (
        scaled_two - normed_two_raw * jnp.mean(scaled_two * normed_two_raw, axis=-1, keepdims=True)
    )
    grad_rows = token_gather(grad_hidden.astype(jnp.bfloat16))
    grad_attended = contract(grad_rows, out_full, 1, 0).astype(jnp.bfloat16)
    grad_query, grad_key, grad_value = attention_backward(
        queries, keys, values, grad_attended, tables
    )
    attention_grads = weight_grads(
        [
            (normed, [(g, 0, head_width) for g in (grad_query, grad_key, grad_value)]),
            (grad_rows, [(attended, 0, head_width)]),
        ],
    )
    attention_grads, grad_query = lax.optimization_barrier((attention_grads, grad_query))
    attention_summed = row_sum(attention_grads)
    attention_halves = exchange_columns(attention_summed)
    grad_normed = product_sum(
        [
            (g, 0, attention_full, which * head_width, head_width)
            for which, g in enumerate((grad_query, grad_key, grad_value))
        ],
        6,
    )
    last_units, grad_normed = lax.optimization_barrier((output_terms[-1][0], grad_normed))
    output_terms[-1] = (last_units, *output_terms[-1][1:])
    layer_output = hidden_state + product_sum(output_terms, 5)
    attention_gain_part = jnp.sum(grad_normed * normed_one, axis=0)
    scaled_one = grad_normed * gain_one
    input_grad = grad_hidden + inv_one * (
        scaled_one - normed_one * jnp.mean(scaled_one * normed_one, axis=-1, keepdims=True)
    )

    def whole_rows(which):
        return jnp.concatenate(
            [
                half[:, which * head_width : (which + 1) * head_width]
                for half in attention_halves
            ],
            axis=1,
        ).astype(jnp.float32)

    def whole_feed_rows(which):
        return jnp.concatenate(
            [
                feed_grads[k][half][:, which * chunk : (which + 1) * chunk]
                for half in range(2)
                for k in range(CHUNKS)
            ],
            axis=1,
        ).astype(jnp.float32)

    gain_sums = sum_everywhere(jnp.stack([attention_gain_part, feed_gain_part]), outer)
    device = lax.axis_index("o")
    for axis in group:
        device = device * 2 + lax.axis_index(axis)
    share = attention_gain.shape[0] // 4
    gain_grads = [
        lax.dynamic_slice_in_dim(gain_sums[which], device * share, share) for which in range(2)
    ]
    return (
        layer_output,
        input_grad,
        *[whole_rows(which) for which in range(4)],
        *[whole_feed_rows(which) for which in range(3)],
        *gain_grads,
    )


def solution(mesh):
    rows, columns = mesh.shape["dp"], mesh.shape["tensor"]
    fine = Mesh(
        mesh.devices.reshape(rows // 2, 2, columns // 2, 2), ("o", "i", "y", "c")
    )
    tokens = P(("o", "i", "y", "c"), None)
    weight = P(("o", "i"), ("y", "c"))
    gain = P(("o", "i"))

    return jax.shard_map(
        per_device,
        mesh=fine,
        in_specs=(tokens, *[weight] * 7, gain, gain, tokens),
        out_specs=(tokens, tokens, *[weight] * 7, P(("o", "i", "y", "c")), P(("o", "i", "y", "c"))),
        check_vma=False,
    )
```

profile of v0, /device:TPU:0, one launch (start us, length us, event | category | flops | bytes accessed | tf_op | source)
XLA Modules:
  0.0 868.7 jit_solution(1366986589438699908)
XLA Ops:
  12.7 11.9 %collective-permute-done = bf16[256,1024]{1,0:T(8,128)(2,1)S(1)} collective-permute-done((bf16[256,1024]{1,0:T(8,128)(2,1)S(1)}, bf16[256,1024]{1,0:T(8,128)(2,1)S(1)}, u32[]{:S(2)}, u32[]{:S(2)}) %collective-permute-start) | collective-permute-done | bytes 524320 | tf_op jit(solution)/shard_map/ppermute | solution.py:592
  30.6 17.0 %collective-permute-done.1 = bf16[256,1536]{1,0:T(8,128)(2,1)S(1)} collective-permute-done((bf16[256,1536]{1,0:T(8,128)(2,1)S(1)}, bf16[256,1536]{1,0:T(8,128)(2,1)S(1)}, u32[]{:S(2)}, u32[]{:S(2)}) %collective-permute-start.1) | collective-permute-done | bytes 786464 | tf_op jit(solution)/shard_map/ppermute | solution.py:592
  51.0 16.5 %collective-permute-done.2 = bf16[256,1536]{1,0:T(8,128)(2,1)S(1)} collective-permute-done((bf16[256,1536]{1,0:T(8,128)(2,1)S(1)}, bf16[256,1536]{1,0:T(8,128)(2,1)S(1)}, u32[]{:S(2)}, u32[]{:S(2)}) %collective-permute-start.2) | collective-permute-done | bytes 786464 | tf_op jit(solution)/shard_map/ppermute | solution.py:592
  69.8 49.6 %opening_gather.1 = (bf16[2048,2048]{1,0:T(8,128)(2,1)}, bf16[8,16,256]{2,1,0:T(8,128)(2,1)}) custom-call(bf16[256,2048]{1,0:T(8,128)(2,1)} %refs_0_.1, bf16[16,256]{1,0:T(8,128)(2,1)} %fusion.18.refs_1_), custom_call_target="tpu_custom_call" | custom-call | bytes 104857600 | tf_op jit(solution)/shard_map/opening_gather/pallas_call | solution.py:146
  119.4 39.8 %token_gather.4.cotangent_ref.refs_2_ = bf16[2048,2048]{1,0:T(8,128)(2,1)} custom-call(bf16[256,2048]{1,0:T(8,128)(2,1)} %refs_0_.2), custom_call_target="tpu_custom_call" | custom-call | bytes 104857600 | tf_op jit(solution)/shard_map/token_gather/pallas_call | solution.py:171
  168.3 8.7 fusion.2.refs_0_
  176.9 11.7 %fusion.3.query_ref.key_ref.value_ref = f32[2048,768]{1,0:T(8,128)} fusion(bf16[2048,2048]{1,0:T(8,128)(2,1)} %fusion.2.refs_0_, bf16[2048,1024]{1,0:T(8,128)(2,1)} %all-gather.4.cloned.1.call-done.refs_1_.refs_3_.refs_4_.refs_5_), kind=kOutput, calls=%fused_computation.5 | convolution fusion | flops 6442450944 | bytes 17825792 | tf_op jit(solution)/shard_map/dot_general | solution.py:21
  188.7 16.4 %attention_forward.1 = (bf16[2048,256]{1,0:T(8,128)(2,1)}, bf16[2048,256]{1,0:T(8,128)(2,1)}, bf16[2048,256]{1,0:T(8,128)(2,1)}, bf16[2048,256]{1,0:T(8,128)(2,1)}) custom-call(f32[2048,768]{1,0:T(8,128)} %fusion.3.query_ref.key_ref.value_ref, f32[2048,768]{1,0:T(8,128)} %fusion.3.query_ref.key_ref.value_ref, f32[2048,768]{1,0:T(8,128)} %fusion.3.query_ref.key_ref.value_ref, ...), custom_call_target="tpu_custom_call" | custom-call | flops 2147483648 | bytes 8388608 | tf_op jit(solution)/shard_map/attention_forward/pallas_call | solution.py:482
  205.1 44.4 %shard_map.194 = f32[256,2048]{1,0:T(8,128)} custom-call(bf16[2048,256]{1,0:T(8,128)(2,1)} %get-tuple-element.35.refs_0_.refs_5_, bf16[2048,1024]{1,0:T(8,128)(2,1)} %all-gather.4.cloned.1.call-done.refs_1_.refs_3_.refs_4_.refs_5_), custom_call_target="tpu_custom_call" | custom-call | flops 2147483648 | bytes 52428800 | tf_op jit(solution)/shard_map/pallas_call | solution.py:357
  252.8 40.2 %token_gather.3.normed_ref.refs_0_ = bf16[2048,2048]{1,0:T(8,128)(2,1)} custom-call(bf16[256,2048]{1,0:T(8,128)(2,1)} %multiply_convert_fusion.refs_0_), custom_call_target="tpu_custom_call" | custom-call | bytes 104857600 | tf_op jit(solution)/shard_map/token_gather/pallas_call | solution.py:171
  293.1 19.4 %feed_units.2.refs_1_.refs_3_.refs_0_ = bf16[2048,1536]{1,0:T(8,128)(2,1)} custom-call(bf16[2048,2048]{1,0:T(8,128)(2,1)} %token_gather.3.normed_ref.refs_0_, bf16[2048,2048]{1,0:T(8,128)(2,1)} %token_gather.4.cotangent_ref.refs_2_, bf16[2048,1536]{1,0:T(8,128)(2,1)} %all-gather.6.cloned.1.call-done.weight_ref.refs_2_), custom_call_target="tpu_custom_call" | custom-call | flops 12884901888 | bytes 29360128 | tf_op jit(solution)/shard_map/feed_units/pallas_call | solution.py:527
  312.5 19.1 %shard_map.195 = bf16[2048,1536]{1,0:T(8,128)(2,1)} custom-call(bf16[2048,2048]{1,0:T(8,128)(2,1)} %token_gather.3.normed_ref.refs_0_, bf16[2048,1536]{1,0:T(8,128)(2,1)} %feed_units.2.refs_1_.refs_3_.refs_0_, bf16[2048,2048]{1,0:T(8,128)(2,1)} %token_gather.4.cotangent_ref.refs_2_, bf16[2048,1536]{1,0:T(8,128)(2,1)} %feed_units.2.refs_1_.refs_3_.refs_0_), custom_call_target="tpu_custom_call" | custom-call | flops 12884901888 | bytes 29360128 | tf_op jit(solution)/shard_map/pallas_call | solution.py:569
  340.0 19.1 %feed_units.3.refs_1_.refs_3_ = bf16[2048,1536]{1,0:T(8,128)(2,1)} custom-call(bf16[2048,2048]{1,0:T(8,128)(2,1)} %token_gather.3.normed_ref.refs_0_, bf16[2048,2048]{1,0:T(8,128)(2,1)} %token_gather.4.cotangent_ref.refs_2_, bf16[2048,1536]{1,0:T(8,128)(2,1)} %all-gather.8.cloned.1.call-done.weight_ref.refs_3_), custom_call_target="tpu_custom_call" | custom-call | flops 12884901888 | bytes 29360128 | tf_op jit(solution)/shard_map/feed_units/pallas_call | solution.py:527
  359.2 19.1 %shard_map.196 = bf16[2048,1536]{1,0:T(8,128)(2,1)} custom-call(bf16[2048,2048]{1,0:T(8,128)(2,1)} %token_gather.3.normed_ref.refs_0_, bf16[2048,1536]{1,0:T(8,128)(2,1)} %feed_units.3.refs_1_.refs_3_, bf16[2048,2048]{1,0:T(8,128)(2,1)} %token_gather.4.cotangent_ref.refs_2_, bf16[2048,1536]{1,0:T(8,128)(2,1)} %feed_units.3.refs_1_.refs_3_), custom_call_target="tpu_custom_call" | custom-call | flops 12884901888 | bytes 29360128 | tf_op jit(solution)/shard_map/pallas_call | solution.py:569
  378.3 57.9 %shard_map.197 = f32[256,2048]{1,0:T(8,128)} custom-call(bf16[2048,1536]{1,0:T(8,128)(2,1)} %feed_units.2.refs_1_.refs_3_.refs_0_, bf16[2048,1536]{1,0:T(8,128)(2,1)} %feed_units.3.refs_1_.refs_3_, bf16[2048,1536]{1,0:T(8,128)(2,1)} %all-gather.6.cloned.1.call-done.weight_ref.refs_2_, bf16[2048,1536]{1,0:T(8,128)(2,1)} %all-gather.8.cloned.1.call-done.weight_ref.refs_3_), custom_call_target="tpu_custom_call" | custom-call | flops 17179869184 | bytes 52428800 | tf_op jit(solution)/shard_map/pallas_call | solution.py:357
  440.3 40.4 %token_gather.5.refs_4_ = bf16[2048,2048]{1,0:T(8,128)(2,1)} custom-call(bf16[256,2048]{1,0:T(8,128)(2,1)} %fusion.23.refs_0_), custom_call_target="tpu_custom_call" | custom-call | bytes 104857600 | tf_op jit(solution)/shard_map/token_gather/pallas_call | solution.py:171
  487.6 30.2 %attention_backward.1 = (bf16[2048,256]{1,0:T(8,128)(2,1)}, bf16[2048,256]{1,0:T(8,128)(2,1)}, bf16[2048,256]{1,0:T(8,128)(2,1)}) custom-call(bf16[2048,256]{1,0:T(8,128)(2,1)} %get-tuple-element.41.query_ref, bf16[2048,256]{1,0:T(8,128)(2,1)} %get-tuple-element.42.key_ref, bf16[2048,256]{1,0:T(8,128)(2,1)} %get-tuple-element.43.value_ref, ...), custom_call_target="tpu_custom_call" | custom-call | flops 5368709120 | bytes 8388608 | tf_op jit(solution)/shard_map/attention_backward/pallas_call | solution.py:497
  517.8 15.6 %shard_map.198 = bf16[2048,1024]{1,0:T(8,128)(2,1)} custom-call(bf16[2048,2048]{1,0:T(8,128)(2,1)} %fusion.2.refs_0_, bf16[2048,256]{1,0:T(8,128)(2,1)} %get-tuple-element.47.refs_1_.refs_0_, bf16[2048,256]{1,0:T(8,128)(2,1)} %get-tuple-element.45.refs_2_.refs_1_, bf16[2048,256]{1,0:T(8,128)(2,1)} %get-tuple-element.46.refs_3_.refs_2_, ...), custom_call_target="tpu_custom_call" | custom-call | flops 8589934592 | bytes 25165824 | tf_op jit(solution)/shard_map/pallas_call | solution.py:569
  534.7 47.2 %shard_map.199 = f32[256,2048]{1,0:T(8,128)} custom-call(bf16[2048,256]{1,0:T(8,128)(2,1)} %get-tuple-element.47.refs_1_.refs_0_, bf16[2048,256]{1,0:T(8,128)(2,1)} %get-tuple-element.45.refs_2_.refs_1_, bf16[2048,256]{1,0:T(8,128)(2,1)} %get-tuple-element.46.refs_3_.refs_2_, bf16[2048,1024]{1,0:T(8,128)(2,1)} %all-gather.4.cloned.1.call-done.refs_1_.refs_3_.refs_4_.refs_5_, ...), custom_call_target="tpu_custom_call" | custom-call | flops 6442450944 | bytes 52428800 | tf_op jit(solution)/shard_map/pallas_call | solution.py:357
  584.8 12.9 %sum_everywhere.1 = f32[32,128]{1,0:T(8,128)} custom-call(f32[32,128]{1,0:T(8,128)} %reshape.100.refs_0_), custom_call_target="tpu_custom_call" | custom-call | tf_op jit(solution)/shard_map/sum_everywhere/pallas_call | solution.py:220
  599.6 48.3 %shard_map.200 = f32[256,2048]{1,0:T(8,128)} custom-call(bf16[2048,1536]{1,0:T(8,128)(2,1)} %feed_units.2.refs_1_.refs_3_.refs_0_, bf16[2048,1536]{1,0:T(8,128)(2,1)} %feed_units.3.refs_1_.refs_3_, bf16[2048,1536]{1,0:T(8,128)(2,1)} %all-gather.6.cloned.1.call-done.weight_ref.refs_2_, bf16[2048,1536]{1,0:T(8,128)(2,1)} %all-gather.8.cloned.1.call-done.weight_ref.refs_3_), custom_call_target="tpu_custom_call" | custom-call | flops 8589934592 | bytes 52428800 | tf_op jit(solution)/shard_map/pallas_call | solution.py:357
  663.0 59.6 %reduce-scatter.6.cloned.1.call-done = bf16[512,1536]{1,0:T(8,128)(2,1)} async-done(((bf16[2048,1536]{1,0:T(8,128)(2,1)}), bf16[512,1536]{1,0:T(8,128)(2,1)}) %reduce-scatter.6.cloned.1.call-update) | async-done | bytes 1572880 | tf_op jit(solution)/shard_map/reduce_scatter | solution.py:603
  728.7 107.3 %reduce-scatter.8.cloned.1.call-done = bf16[512,1536]{1,0:T(8,128)(2,1)} async-done(((bf16[2048,1536]{1,0:T(8,128)(2,1)}), bf16[512,1536]{1,0:T(8,128)(2,1)}) %reduce-scatter.8.cloned.1.call-update) | async-done | bytes 1572880 | tf_op jit(solution)/shard_map/reduce_scatter | solution.py:603
  839.2 17.3 %collective-permute-done.5 = bf16[256,1536]{1,0:T(8,128)(2,1)S(1)} collective-permute-done((bf16[256,1536]{1,0:T(8,128)(2,1)S(1)}, bf16[256,1536]{1,0:T(8,128)(2,1)S(1)}, u32[]{:S(2)}, u32[]{:S(2)}) %collective-permute-start.5) | collective-permute-done | bytes 786464 | tf_op jit(solution)/shard_map/ppermute | solution.py:610
  (100 shorter events, 84.4 us)
Async XLA Ops:
  7.2 169.8 %all-gather.4.cloned.1.call-start = ((), (), s32[]{:S(2)}) async-start(), calls=%async_computation.3 | async-start | bytes 5242880 | tf_op jit(solution)/shard_map/all_gather | solution.py:599
  9.7 15.0 %collective-permute-start = (bf16[256,1024]{1,0:T(8,128)(2,1)S(1)}, bf16[256,1024]{1,0:T(8,128)(2,1)S(1)}, u32[]{:S(2)}, u32[]{:S(2)}) collective-permute-start(bf16[256,1024]{1,0:T(8,128)(2,1)S(1)} %broadcast_select_fusion.16), channel_id=1, source_target_pairs={{0,4},{4,0},{1,5},{5,1},{2,6},{6,2},{3,7},{7,3},{8,12},{12,8},{9,1... | collective-permute-start | bytes 1572872 | tf_op jit(solution)/shard_map/ppermute | solution.py:592
  24.9 1.6 copy-start.5
  25.9 1.3 copy-start.7
  25.9 267.1 %all-gather.6.cloned.1.call-start = ((), (), s32[]{:S(2)}) async-start(), calls=%async_computation.4 | async-start | bytes 7864320 | tf_op jit(solution)/shard_map/all_gather | solution.py:599
  28.8 18.8 %collective-permute-start.1 = (bf16[256,1536]{1,0:T(8,128)(2,1)S(1)}, bf16[256,1536]{1,0:T(8,128)(2,1)S(1)}, u32[]{:S(2)}, u32[]{:S(2)}) collective-permute-start(bf16[256,1536]{1,0:T(8,128)(2,1)S(1)} %broadcast_select_fusion.10), channel_id=1, source_target_pairs={{0,4},{4,0},{1,5},{5,1},{2,6},{6,2},{3,7},{7,3},{8,12},{12,8},{9,1... | collective-permute-start | bytes 2359304 | tf_op jit(solution)/shard_map/ppermute | solution.py:592
  49.2 290.8 %all-gather.8.cloned.1.call-start = ((), (), s32[]{:S(2)}) async-start(), calls=%async_computation.5 | async-start | bytes 7864320 | tf_op jit(solution)/shard_map/all_gather | solution.py:599
  49.5 18.0 %collective-permute-start.2 = (bf16[256,1536]{1,0:T(8,128)(2,1)S(1)}, bf16[256,1536]{1,0:T(8,128)(2,1)S(1)}, u32[]{:S(2)}, u32[]{:S(2)}) collective-permute-start(bf16[256,1536]{1,0:T(8,128)(2,1)S(1)} %broadcast_select_fusion.6), channel_id=1, source_target_pairs={{0,4},{4,0},{1,5},{5,1},{2,6},{6,2},{3,7},{7,3},{8,12},{12,8},{9,1... | collective-permute-start | bytes 2359304 | tf_op jit(solution)/shard_map/ppermute | solution.py:592
  67.9 1.3 copy-start.8
  67.9 1.4 copy-start.9
  69.1 578.8 %reduce-scatter.4.cloned.1.call-start = ((), (), s32[]{:S(2)}) async-start(), calls=%async_computation.6 | async-start | bytes 5242880 | tf_op jit(solution)/shard_map/reduce_scatter | solution.py:603
  205.1 44.4 %copy-start.1 = (bf16[256,2048]{1,0:T(8,128)(2,1)S(1)}, bf16[256,2048]{1,0:T(8,128)(2,1)}, u32[]{:S(2)}) copy-start(bf16[256,2048]{1,0:T(8,128)(2,1)} %refs_0_.1) | copy-start | bytes 3145732
  436.2 2.3 copy-start
  436.2 2.5 copy-start.2
  533.5 189.1 %reduce-scatter.6.cloned.1.call-start = ((), (), s32[]{:S(2)}) async-start(), calls=%async_computation.7 | async-start | bytes 7864320 | tf_op jit(solution)/shard_map/reduce_scatter | solution.py:603
  534.1 302.0 %reduce-scatter.8.cloned.1.call-start = ((), (), s32[]{:S(2)}) async-start(), calls=%async_computation.8 | async-start | bytes 7864320 | tf_op jit(solution)/shard_map/reduce_scatter | solution.py:603
  649.0 13.6 %copy-start.6 = (bf16[512,1024]{1,0:T(8,128)(2,1)S(1)}, bf16[512,1024]{1,0:T(8,128)(2,1)}, u32[]{:S(2)}) copy-start(bf16[512,1024]{1,0:T(8,128)(2,1)} %reduce-scatter.4.cloned.1.call-done) | copy-start | bytes 3145732
  649.0 13.6 %collective-permute-start.3 = (bf16[256,1024]{1,0:T(8,128)(2,1)S(1)}, bf16[256,1024]{1,0:T(8,128)(2,1)S(1)}, u32[]{:S(2)}, u32[]{:S(2)}) collective-permute-start(bf16[256,1024]{1,0:T(8,128)(2,1)S(1)} %constant_dynamic-slice_fusion.2), channel_id=1, source_target_pairs={{0,4},{4,0},{1,5},{5,1},{2,6},{6,2},{3,7},{7,3},{8,12},{12,8},{9,1... | collective-permute-start | bytes 1572872 | tf_op jit(solution)/shard_map/ppermute | solution.py:610
  723.7 115.0 %collective-permute-start.4 = (bf16[256,1536]{1,0:T(8,128)(2,1)S(1)}, bf16[256,1536]{1,0:T(8,128)(2,1)S(1)}, u32[]{:S(2)}, u32[]{:S(2)}) collective-permute-start(bf16[256,1536]{1,0:T(8,128)(2,1)S(1)} %constant_dynamic-slice_fusion.1), channel_id=1, source_target_pairs={{0,4},{4,0},{1,5},{5,1},{2,6},{6,2},{3,7},{7,3},{8,12},{12,8},{9,1... | collective-permute-start | bytes 2359304 | tf_op jit(solution)/shard_map/ppermute | solution.py:610
  726.2 112.6 %copy-start.4 = (bf16[512,1536]{1,0:T(8,128)(2,1)S(1)}, bf16[512,1536]{1,0:T(8,128)(2,1)}, u32[]{:S(2)}) copy-start(bf16[512,1536]{1,0:T(8,128)(2,1)} %reduce-scatter.6.cloned.1.call-done) | copy-start | bytes 4718596
  837.2 19.3 %collective-permute-start.5 = (bf16[256,1536]{1,0:T(8,128)(2,1)S(1)}, bf16[256,1536]{1,0:T(8,128)(2,1)S(1)}, u32[]{:S(2)}, u32[]{:S(2)}) collective-permute-start(bf16[256,1536]{1,0:T(8,128)(2,1)S(1)} %constant_dynamic-slice_fusion), channel_id=1, source_target_pairs={{0,4},{4,0},{1,5},{5,1},{2,6},{6,2},{3,7},{7,3},{8,12},{12,8},{9,1... | collective-permute-start | bytes 2359304 | tf_op jit(solution)/shard_map/ppermute | solution.py:610
  839.1 17.4 %copy-start.3 = (bf16[512,1536]{1,0:T(8,128)(2,1)S(1)}, bf16[512,1536]{1,0:T(8,128)(2,1)}, u32[]{:S(2)}) copy-start(bf16[512,1536]{1,0:T(8,128)(2,1)} %reduce-scatter.8.cloned.1.call-done) | copy-start | bytes 4718596
Sparse Core Ops, SparseCore 0:
  26.1 82.2 all-gather.3
  110.5 113.8 all-gather.5
  226.5 113.5 all-gather.7
  533.6 75.4 reduce-scatter.3
  611.2 111.2 reduce-scatter.5
  724.7 111.2 reduce-scatter.7
where the time goes:
time: 875 us; the launch traced here: 869 us
  Pallas kernels  520 us (59%)
  waiting for transfers between devices  245 us (28%)
  other arithmetic  48.2 us (6%)
  matrix products  18.6 us (2%)
  between operations  14.7 us (2%)
  local copies, waits for them, and re-layouts  11.3 us (1%)
  starting transfers between devices  11.2 us (1%)
    pallas_call x4, Pallas kernels, product_sum(): pl.pallas_call(lambda *refs: scatter_kernel(windows, *refs), in_specs=[pl...  198 us
    reduce_scatter x3, waiting for transfers between devices, row_sum(): return lax.psum_scatter(partial_value, 'o', scatter_dimension=0, tiled=True)  167 us
    pallas_call x3, Pallas kernels, token_gather(): pl.pallas_call(lambda *refs: gather_kernel(1, *refs), in_specs=[pl.BlockS...  120 us
    pallas_call x3, Pallas kernels, weight_grads(): pl.pallas_call(kernel, grid=(width // tile,), in_specs=specs, out_specs=p...  53.8 us
    pallas_call x1, Pallas kernels, opening_gather(): pl.pallas_call(lambda *refs: opening_kernel(outer, *refs), in_specs=[vmem...  49.6 us
    ppermute x3, waiting for transfers between devices, exchange_rows(): other = lax.ppermute(jnp.where(side == 0, high, low), 'i', swap)  45.4 us
    pallas_call x2, Pallas kernels, feed_units(): pl.pallas_call(feed_kernel, grid=(rows // tile,), in_specs=[tokens, token...  38.5 us
    pallas_call x1, Pallas kernels, attention_backward(): pl.pallas_call(backward_kernel, grid=(rows // LEN, width // PAIR), in_spe...  30.2 us
  transfers between devices with their start and end apart: 12, of which 8 were waited for; matrix products, arithmetic and copies ran while one was open for 7% of the time, Pallas kernels for 39%

commit v1 on v0

--- a/solution.py
+++ b/solution.py
@@ -182,202 +182,340 @@
     )(array)
 
 
-def total_kernel(outer, part_ref, total_ref, held, stages, semaphores, row_semaphores):
-    greet_partners(outer)
-    started = []
-    source, value = part_ref, part_ref[...]
-    for step, axis in enumerate(group):
-        copy = send_along(axis, source, held.at[step], semaphores, step)
-        copy.start()
-        started.append(copy)
-        copy.wait_recv()
-        value = value + held[step]
-        stages[step] = value
-        source = stages.at[step]
-    copies = []
-    for shift in range(1, outer):
-        copy = pltpu.make_async_remote_copy(
-            src_ref=source,
-            dst_ref=held.at[2 + shift],
-            send_sem=row_semaphores.at[0, shift],
-            recv_sem=row_semaphores.at[1, shift],
-            device_id=row_partner(shift, outer),
-            device_id_type=MESH,
+class TokenSum:
+    def __init__(self, windows, lefts, rights, total, scratch):
+        self.windows, self.lefts, self.rights, self.total = windows, lefts, rights, total
+        (
+            self.left_held,
+            self.right_held,
+            self.core_out,
+            self.core_in,
+            self.sums,
+            self.first_i,
+            self.first_y,
+            self.second_i,
+            self.second_y,
+            self.left_semaphores,
+            self.right_semaphores,
+            self.semaphores,
+        ) = scratch
+        rows, _ = total.shape
+        half = rows // 2
+        self.top, self.bottom = top, bottom = pl.ds(0, half), pl.ds(half, half)
+        sums, first_i, first_y = self.sums, self.first_i, self.first_y
+        plan = {
+            "i1": ("i", sums.at[0, top, :], first_i.at[1], 4),
+            "y1": ("y", sums.at[0, bottom, :], first_y.at[1], 5),
+            "i0": ("i", sums.at[1, top, :], first_i.at[0], 6),
+            "y0": ("y", sums.at[2, bottom, :], first_y.at[0], 7),
+            "i2": ("i", sums.at[1, bottom, :], self.second_i, 8),
+            "y2": ("y", sums.at[2, top, :], self.second_y, 9),
+        }
+        self.copies = {
+            name: send_along(axis, source, target, self.semaphores, slot)
+            for name, (axis, source, target, slot) in plan.items()
+        }
+
+    def core_copy(self, r):
+        return send_along("c", self.core_out.at[r], self.core_in.at[r], self.semaphores, r)
+
+    def right_copies(self):
+        edge = 0
+        for which, (_, start, depth) in enumerate(self.windows):
+            yield pltpu.make_async_copy(
+                self.rights[which].at[:, pl.ds(start, depth)],
+                self.right_held.at[:, pl.ds(edge, depth)],
+                self.right_semaphores.at[which],
+            )
+            edge += depth
+
+    def left_copies(self, step, first):
+        rows, edge = self.total.shape[0], 0
+        for which, (start, _, depth) in enumerate(self.windows):
+            yield pltpu.make_async_copy(
+                self.lefts[which].at[pl.ds(first, rows), pl.ds(start, depth)],
+                self.left_held.at[step, :, pl.ds(edge, depth)],
+                self.left_semaphores.at[step, which],
+            )
+            edge += depth
+
+    def load(self):
+        for copy in self.right_copies():
+            copy.start()
+        rows = self.total.shape[0]
+        for r, flips in enumerate((("i", "y"), ("i",), ("y",), ())):
+            for mine, axes in enumerate((flips + ("c",), flips)):
+                for copy in self.left_copies(2 * r + mine, first_row(axes, rows)):
+                    copy.start()
+
+    def add_to(self, r, part, arrived):
+        self.sums[r, part, :] = (
+            self.sums[r, part, :].astype(jnp.float32) + arrived.astype(jnp.float32)
+        ).astype(jnp.bfloat16)
+
+    def second(self):
+        self.copies["y1"].wait_recv()
+        self.add_to(1, self.bottom, self.first_y[1])
+        self.copies["i2"].start()
+        self.copies["i1"].wait_recv()
+        self.add_to(2, self.top, self.first_i[1])
+        self.copies["y2"].start()
+
+    def run(self, second_inside):
+        width = self.total.shape[1]
+        tile = 512
+        for copy in self.right_copies():
+            copy.wait()
+
+        def product(step, t):
+            columns = pl.ds(pl.multiple_of(t * tile, tile), tile)
+            return columns, contract(
+                self.left_held[step], self.right_held[columns, :], 1, 1
+            )
+
+        def one_relation(r, carry):
+            for copy in self.left_copies(2 * r, 0):
+                copy.wait()
+
+            def sibling_tile(t, inner):
+                columns, value = product(2 * r, t)
+                self.core_out[r, :, columns] = value.astype(jnp.bfloat16)
+                return inner
+
+            lax.fori_loop(0, width // tile, sibling_tile, 0)
+            self.core_copy(r).start()
+            for copy in self.left_copies(2 * r + 1, 0):
+                copy.wait()
+            self.core_copy(r).wait_recv()
+
+            def own_tile(t, inner):
+                columns, value = product(2 * r + 1, t)
+                value = value + self.core_in[r, :, columns].astype(jnp.float32)
+
+                @pl.when(r < 3)
+                def _():
+                    self.sums[r, :, columns] = value.astype(jnp.bfloat16)
+
+                @pl.when(r == 3)
+                def _():
+                    self.total[:, columns] = value
+
+                return inner
+
+            lax.fori_loop(0, width // tile, own_tile, 0)
+
+            @pl.when(r == 0)
+            def _():
+                self.copies["i1"].start()
+                self.copies["y1"].start()
+
+            @pl.when(r == 1)
+            def _():
+                self.copies["i0"].start()
+
+            @pl.when(r == 2)
+            def _():
+                self.copies["y0"].start()
+                if second_inside:
+                    self.second()
+
+            return carry
+
+        lax.fori_loop(0, 4, one_relation, 0)
+
+    def finish(self):
+        self.copies["i0"].wait_recv()
+        self.total[self.top, :] += self.first_i[0].astype(jnp.float32)
+        self.copies["y0"].wait_recv()
+        self.total[self.bottom, :] += self.first_y[0].astype(jnp.float32)
+        self.copies["y2"].wait_recv()
+        self.total[self.top, :] += self.second_y[...].astype(jnp.float32)
+        self.copies["i2"].wait_recv()
+        self.total[self.bottom, :] += self.second_i[...].astype(jnp.float32)
+
+    def drain(self):
+        for copy in self.copies.values():
+            copy.wait_send()
+        for r in range(4):
+            self.core_copy(r).wait_send()
+
+
+def sum_scratch(terms):
+    rows, width = terms[0][0].shape[0] // 8, terms[0][2].shape[0]
+    half, depth, count = rows // 2, sum(term[4] for term in terms), len(terms)
+    return [
+        pltpu.VMEM((8, rows, depth), jnp.bfloat16),
+        pltpu.VMEM((width, depth), jnp.bfloat16),
+        pltpu.VMEM((4, rows, width), jnp.bfloat16),
+        pltpu.VMEM((4, rows, width), jnp.bfloat16),
+        pltpu.VMEM((4, rows, width), jnp.bfloat16),
+        pltpu.VMEM((2, half, width), jnp.bfloat16),
+        pltpu.VMEM((2, half, width), jnp.bfloat16),
+        pltpu.VMEM((half, width), jnp.bfloat16),
+        pltpu.VMEM((half, width), jnp.bfloat16),
+        pltpu.SemaphoreType.DMA((8, count)),
+        pltpu.SemaphoreType.DMA((count,)),
+        pltpu.SemaphoreType.DMA((2, 10)),
+    ]
+
+
+def sum_operands(terms):
+    return [term[0] for term in terms] + [term[2] for term in terms]
+
+
+def sum_steps(terms, operands, total, scratch):
+    windows = [(term[1], term[3], term[4]) for term in terms]
+    return TokenSum(windows, operands[: len(terms)], operands[len(terms) :], total, scratch)
+
+
+def sum_flops(terms):
+    return sum(2 * t[0].shape[0] * t[2].shape[0] * t[4] for t in terms)
+
+
+def product_sum(terms, number):
+    rows, width = terms[0][0].shape[0] // 8, terms[0][2].shape[0]
+    count = 2 * len(terms)
+
+    def kernel(*refs):
+        steps = sum_steps(terms, refs[:count], refs[count], refs[count + 1 :])
+        steps.load()
+        greet_partners()
+        steps.run(True)
+        steps.finish()
+        steps.drain()
+
+    return pl.pallas_call(
+        kernel,
+        in_specs=[pl.BlockSpec(memory_space=pl.ANY)] * count,
+        out_specs=pl.BlockSpec(memory_space=pltpu.VMEM),
+        out_shape=jax.ShapeDtypeStruct((rows, width), jnp.float32),
+        scratch_shapes=sum_scratch(terms),
+        compiler_params=pltpu.CompilerParams(collective_id=number, has_side_effects=True),
+        cost_estimate=pl.CostEstimate(
+            flops=sum_flops(terms), bytes_accessed=100 * rows * width, transcendentals=0
+        ),
+    )(*sum_operands(terms))
+
+
+def input_gradient(terms, inputs, grad_hidden, gain):
+    rows, width = inputs.shape
+    count = 2 * len(terms)
+    tile = 32
+
+    def kernel(*refs):
+        input_ref, grad_hidden_ref, gain_ref, grad_out, part_out = refs[count : count + 5]
+        steps = sum_steps(terms, refs[:count], grad_out, refs[count + 5 :])
+        steps.load()
+        greet_partners()
+        steps.run(True)
+        steps.finish()
+
+        def one_tile(t, part):
+            span = pl.ds(pl.multiple_of(t * tile, tile), tile)
+            values = input_ref[span, :].astype(jnp.float32)
+            inverse = inverse_rms(values)
+            normed = values * inverse
+            grad_normed = grad_out[span, :]
+            scaled = grad_normed * gain_ref[...]
+            mean = jnp.mean(scaled * normed, axis=-1, keepdims=True)
+            grad_out[span, :] = grad_hidden_ref[span, :] + inverse * (scaled - normed * mean)
+            return part + jnp.sum(grad_normed * normed, axis=0, keepdims=True)
+
+        part_out[...] = lax.fori_loop(
+            0, rows // tile, one_tile, jnp.zeros((1, width), jnp.float32)
         )
-        copy.start()
-        copies.append(copy)
-    for shift, copy in enumerate(copies):
-        copy.wait_recv()
-        value = value + held[3 + shift]
-    total_ref[...] = value
-    for copy in started + copies:
-        copy.wait_send()
-
-
-def sum_everywhere(part, outer):
-    folded = part.reshape(-1, 128)
-    spec = pl.BlockSpec(memory_space=pltpu.VMEM)
+        steps.drain()
+
+    vmem, hbm = pl.BlockSpec(memory_space=pltpu.VMEM), pl.BlockSpec(memory_space=pl.ANY)
     return pl.pallas_call(
-        lambda *refs: total_kernel(outer, *refs),
-        in_specs=[spec],
-        out_specs=spec,
-        out_shape=jax.ShapeDtypeStruct(folded.shape, jnp.float32),
+        kernel,
+        in_specs=[hbm] * count + [vmem] * 3,
+        out_specs=[vmem] * 2,
+        out_shape=[
+            jax.ShapeDtypeStruct((rows, width), jnp.float32),
+            jax.ShapeDtypeStruct((1, width), jnp.float32),
+        ],
+        scratch_shapes=sum_scratch(terms),
+        compiler_params=pltpu.CompilerParams(collective_id=6, has_side_effects=True),
+        cost_estimate=pl.CostEstimate(
+            flops=sum_flops(terms), bytes_accessed=150 * rows * width, transcendentals=rows
+        ),
+        name="input_gradient",
+    )(*sum_operands(terms), inputs, grad_hidden, gain.reshape(1, width))
+
+
+def closing(terms, hidden, parts, outer):
+    rows, width = hidden.shape
+    count = 2 * len(terms)
+
+    def kernel(*refs):
+        hidden_ref, part_ref, layer_out, total_out = refs[count : count + 4]
+        scratch = refs[count + 4 :]
+        held, stages, semaphores, row_semaphores = scratch[-4:]
+        output = sum_steps(terms, refs[:count], layer_out, scratch[:-4])
+        output.load()
+        greet_partners(outer)
+        started = []
+
+        def pass_on(step, source):
+            copy = send_along(group[step], source, held.at[step], semaphores, step)
+            copy.start()
+            started.append(copy)
+
+        pass_on(0, part_ref)
+        output.run(False)
+        value = part_ref[...]
+        for step in range(3):
+            started[step].wait_recv()
+            value = value + held[step]
+            stages[step] = value
+            if step < 2:
+                pass_on(step + 1, stages.at[step])
+        for shift in range(1, outer):
+            copy = pltpu.make_async_remote_copy(
+                src_ref=stages.at[2],
+                dst_ref=held.at[2 + shift],
+                send_sem=row_semaphores.at[0, shift],
+                recv_sem=row_semaphores.at[1, shift],
+                device_id=row_partner(shift, outer),
+                device_id_type=MESH,
+            )
+            copy.start()
+            started.append(copy)
+        output.second()
+        output.finish()
+        layer_out[...] += hidden_ref[...]
+        value = stages[2]
+        for shift in range(1, outer):
+            started[2 + shift].wait_recv()
+            value = value + held[2 + shift]
+        total_out[...] = value
+        for copy in started:
+            copy.wait_send()
+        output.drain()
+
+    vmem, hbm = pl.BlockSpec(memory_space=pltpu.VMEM), pl.BlockSpec(memory_space=pl.ANY)
+    return pl.pallas_call(
+        kernel,
+        in_specs=[hbm] * count + [vmem] * 2,
+        out_specs=[vmem] * 2,
+        out_shape=[
+            jax.ShapeDtypeStruct((rows, width), jnp.float32),
+            jax.ShapeDtypeStruct(parts.shape, jnp.float32),
+        ],
         scratch_shapes=[
-            pltpu.VMEM((2 + outer, *folded.shape), jnp.float32),
-            pltpu.VMEM((3, *folded.shape), jnp.float32),
+            *sum_scratch(terms),
+            pltpu.VMEM((2 + outer, *parts.shape), jnp.float32),
+            pltpu.VMEM((3, *parts.shape), jnp.float32),
             pltpu.SemaphoreType.DMA((2, 3)),
             pltpu.SemaphoreType.DMA((2, max(outer, 2))),
         ],
-        compiler_params=pltpu.CompilerParams(collective_id=7, has_side_effects=True),
-        name="sum_everywhere",
-    )(folded).reshape(part.shape)
-
-
-def scatter_kernel(windows, *refs):
-    count = len(windows)
-    lefts, rights, total = refs[:count], refs[count : 2 * count], refs[2 * count]
-    (
-        left_held,
-        right_held,
-        core_out,
-        core_in,
-        sums,
-        first_i,
-        first_y,
-        second_i,
-        second_y,
-        left_semaphores,
-        right_semaphores,
-        semaphores,
-    ) = refs[2 * count + 1 :]
-    rows, width = total.shape
-    half = rows // 2
-    tile = 512
-    relations = (("i", "y"), ("i",), ("y",), ())
-    order = [(r, mine) for r in range(4) for mine in (False, True)]
-
-    loads = []
-    edge = 0
-    for which, (left_start, right_start, depth) in enumerate(windows):
-        copy = pltpu.make_async_copy(
-            rights[which].at[:, pl.ds(right_start, depth)],
-            right_held.at[:, pl.ds(edge, depth)],
-            right_semaphores.at[which],
-        )
-        copy.start()
-        loads.append(copy)
-        edge += depth
-    left_loads = []
-    for step, (r, mine) in enumerate(order):
-        flips = relations[r] if mine else relations[r] + ("c",)
-        start = first_row(flips, rows)
-        edge = 0
-        row = []
-        for which, (left_start, right_start, depth) in enumerate(windows):
-            copy = pltpu.make_async_copy(
-                lefts[which].at[pl.ds(start, rows), pl.ds(left_start, depth)],
-                left_held.at[step, :, pl.ds(edge, depth)],
-                left_semaphores.at[step, which],
-            )
-            copy.start()
-            row.append(copy)
-            edge += depth
-        left_loads.append(row)
-    greet_partners()
-    for copy in loads:
-        copy.wait()
-
-    top, bottom = pl.ds(0, half), pl.ds(half, half)
-    started = []
-
-    def send(axis, source, target, slot):
-        copy = send_along(axis, source, target, semaphores, slot)
-        copy.start()
-        started.append(copy)
-        return copy
-
-    core_copies, copies = [], {}
-    for step, (r, mine) in enumerate(order):
-        for copy in left_loads[step]:
-            copy.wait()
-        if mine:
-            core_copies[r].wait_recv()
-
-        def one_tile(t, carry):
-            columns = pl.ds(pl.multiple_of(t * tile, tile), tile)
-            part = contract(left_held[step], right_held[columns, :], 1, 1)
-            if not mine:
-                core_out[r, :, columns] = part.astype(jnp.bfloat16)
-            elif r < 3:
-                sums[r, :, columns] = (part + core_in[r, :, columns].astype(jnp.float32)).astype(
-                    jnp.bfloat16
-                )
-            else:
-                total[:, columns] = part + core_in[r, :, columns].astype(jnp.float32)
-            return carry
-
-        lax.fori_loop(0, width // tile, one_tile, 0)
-        if not mine:
-            core_copies.append(send("c", core_out.at[r], core_in.at[r], r))
-        elif r == 0:
-            copies["i1"] = send("i", sums.at[0, top, :], first_i.at[1], 4)
-            copies["y1"] = send("y", sums.at[0, bottom, :], first_y.at[1], 5)
-        elif r == 1:
-            copies["i0"] = send("i", sums.at[1, top, :], first_i.at[0], 6)
-        elif r == 2:
-            copies["y0"] = send("y", sums.at[2, bottom, :], first_y.at[0], 7)
-            copies["y1"].wait_recv()
-            sums[1, bottom, :] = (
-                sums[1, bottom, :].astype(jnp.float32) + first_y[1].astype(jnp.float32)
-            ).astype(jnp.bfloat16)
-            copies["i2"] = send("i", sums.at[1, bottom, :], second_i, 8)
-            copies["i1"].wait_recv()
-            sums[2, top, :] = (
-                sums[2, top, :].astype(jnp.float32) + first_i[1].astype(jnp.float32)
-            ).astype(jnp.bfloat16)
-            copies["y2"] = send("y", sums.at[2, top, :], second_y, 9)
-    copies["i0"].wait_recv()
-    total[top, :] += first_i[0].astype(jnp.float32)
-    copies["y0"].wait_recv()
-    total[bottom, :] += first_y[0].astype(jnp.float32)
-    copies["y2"].wait_recv()
-    total[top, :] += second_y[...].astype(jnp.float32)
-    copies["i2"].wait_recv()
-    total[bottom, :] += second_i[...].astype(jnp.float32)
-    for copy in started:
-        copy.wait_send()
-
-
-def product_sum(terms, number):
-    rows, width = terms[0][0].shape[0] // 8, terms[0][2].shape[0]
-    half = rows // 2
-    count = len(terms)
-    depth = sum(term[4] for term in terms)
-    windows = [(term[1], term[3], term[4]) for term in terms]
-    return pl.pallas_call(
-        lambda *refs: scatter_kernel(windows, *refs),
-        in_specs=[pl.BlockSpec(memory_space=pl.ANY)] * (2 * count),
-        out_specs=pl.BlockSpec(memory_space=pltpu.VMEM),
-        out_shape=jax.ShapeDtypeStruct((rows, width), jnp.float32),
-        scratch_shapes=[
-            pltpu.VMEM((8, rows, depth), jnp.bfloat16),
-            pltpu.VMEM((width, depth), jnp.bfloat16),
-            pltpu.VMEM((4, rows, width), jnp.bfloat16),
-            pltpu.VMEM((4, rows, width), jnp.bfloat16),
-            pltpu.VMEM((3, rows, width), jnp.bfloat16),
-            pltpu.VMEM((2, half, width), jnp.bfloat16),
-            pltpu.VMEM((2, half, width), jnp.bfloat16),
-            pltpu.VMEM((half, width), jnp.bfloat16),
-            pltpu.VMEM((half, width), jnp.bfloat16),
-            pltpu.SemaphoreType.DMA((8, count)),
-            pltpu.SemaphoreType.DMA((count,)),
-            pltpu.SemaphoreType.DMA((2, 10)),
-        ],
-        compiler_params=pltpu.CompilerParams(collective_id=number, has_side_effects=True),
+        compiler_params=pltpu.CompilerParams(collective_id=5, has_side_effects=True),
         cost_estimate=pl.CostEstimate(
-            flops=16 * rows * depth * width, bytes_accessed=100 * rows * width, transcendentals=0
+            flops=sum_flops(terms), bytes_accessed=150 * rows * width, transcendentals=0
         ),
-    )(*[term[0] for term in terms], *[term[2] for term in terms])
+        name="closing",
+    )(*sum_operands(terms), hidden, parts)
 
 
 def rope_tables():
@@ -610,6 +748,12 @@
     other = lax.ppermute(
         lax.dynamic_slice_in_dim(summed, (1 - side) * rows, rows, axis=0), "i", swap
     )
+    return kept, other
+
+
+def in_order(halves):
+    kept, other = halves
+    side = lax.axis_index("i")
     return jnp.where(side == 0, kept, other), jnp.where(side == 0, other, kept)
 
 
@@ -645,14 +789,12 @@
         feed_rows = exchange_rows((gate_weight, up_weight, down_weight), k * chunk, chunk)
         feed_full.append(row_gather(feed_rows))
     inputs_all, gains = opening_gather(layer_input, jnp.stack([attention_gain, feed_gain]), outer)
-    inputs_all, late = lax.optimization_barrier((inputs_all, out_cotangent))
-    cotangents = token_gather(late)
     gain_one, gain_two = [g.astype(jnp.float32) for g in gains]
     inputs_all = inputs_all.astype(jnp.float32)
     normed = (inputs_all * inverse_rms(inputs_all) * gain_one).astype(jnp.bfloat16)
+    normed, tables, late = lax.optimization_barrier((normed, tables, out_cotangent))
+    cotangents = token_gather(late)
     inputs = layer_input.astype(jnp.float32)
-    inv_one = inverse_rms(inputs)
-    normed_one = inputs * inv_one
 
     mixed = contract(normed, attention_full[:, : 3 * head_width], 1, 0)
     queries, keys, values, attended = attention_forward(mixed, tables)
@@ -682,7 +824,7 @@
         output_terms.append((units, 2 * chunk, feed_full[k], 2 * chunk, chunk))
 
     grad_normed_two = product_sum(grad_terms, 4)
-    feed_gain_part = jnp.sum(grad_normed_two * normed_two_raw, axis=0)
+    feed_gain_part = jnp.sum(grad_normed_two * normed_two_raw, axis=0, keepdims=True)
     scaled_two = grad_normed_two * gain_two
     grad_hidden = out_cotangent.astype(jnp.float32) + inv_two * (
         scaled_two - normed_two_raw * jnp.mean(scaled_two * normed_two_raw, axis=-1, keepdims=True)
@@ -701,42 +843,32 @@
     attention_grads, grad_query = lax.optimization_barrier((attention_grads, grad_query))
     attention_summed = row_sum(attention_grads)
     attention_halves = exchange_columns(attention_summed)
-    grad_normed = product_sum(
+    input_grad, attention_gain_part = input_gradient(
         [
             (g, 0, attention_full, which * head_width, head_width)
             for which, g in enumerate((grad_query, grad_key, grad_value))
         ],
-        6,
-    )
-    last_units, grad_normed = lax.optimization_barrier((output_terms[-1][0], grad_normed))
-    output_terms[-1] = (last_units, *output_terms[-1][1:])
-    layer_output = hidden_state + product_sum(output_terms, 5)
-    attention_gain_part = jnp.sum(grad_normed * normed_one, axis=0)
-    scaled_one = grad_normed * gain_one
-    input_grad = grad_hidden + inv_one * (
-        scaled_one - normed_one * jnp.mean(scaled_one * normed_one, axis=-1, keepdims=True)
-    )
-
-    def whole_rows(which):
+        layer_input,
+        grad_hidden,
+        gain_one,
+    )
+    parts = jnp.concatenate([attention_gain_part, feed_gain_part, jnp.zeros((6, feed_gain_part.shape[1]))])
+    layer_output, gain_sums = closing(output_terms, hidden_state, parts, outer)
+
+    def whole_rows(halves, which, width):
         return jnp.concatenate(
             [
-                half[:, which * head_width : (which + 1) * head_width]
-                for half in attention_halves
+                half[k][:, which * width : (which + 1) * width]
+                for half in zip(*halves)
+                for k in range(len(halves))
             ],
             axis=1,
         ).astype(jnp.float32)
 
-    def whole_feed_rows(which):
-        return jnp.concatenate(
-            [
-                feed_grads[k][half][:, which * chunk : (which + 1) * chunk]
-                for half in range(2)
-                for k in range(CHUNKS)
-            ],
-            axis=1,
-        ).astype(jnp.float32)
-
-    gain_sums = sum_everywhere(jnp.stack([attention_gain_part, feed_gain_part]), outer)
+    feed_halves = [in_order(halves) for halves in feed_grads]
+    feed_rows = [whole_rows(feed_halves, which, chunk) for which in range(3)]
+    attention_halves = [in_order(attention_halves)]
+    attention_rows = [whole_rows(attention_halves, which, head_width) for which in range(4)]
     device = lax.axis_index("o")
     for axis in group:
         device = device * 2 + lax.axis_index(axis)
@@ -747,8 +879,8 @@
     return (
         layer_output,
         input_grad,
-        *[whole_rows(which) for which in range(4)],
-        *[whole_feed_rows(which) for which in range(3)],
+        *attention_rows,
+        *feed_rows,
         *gain_grads,
     )
 

time: 875 us -> 884 us (1.010)
  waiting for transfers between devices: 245 us -> 255 us
    pallas_call x5 -> x4, Pallas kernels: 211 us -> 210 us  [the longest x2 102 us: product_sum(): pl.pallas_call(kernel, in_specs=[pl.BlockSpec(memory_space=pl.ANY)] * cou...]
  transfers between devices with their start and end apart: 12 -> 12, of which waited for: 8 -> 8; matrix products, arithmetic and copies ran while one was open for 7% -> 6% of each run, Pallas kernels for 39% -> 38%
where the time goes in v1:
time: 884 us; the launch traced here: 877 us
  Pallas kernels  520 us (59%)
  waiting for transfers between devices  255 us (29%)
  other arithmetic  43 us (5%)
  matrix products  18.7 us (2%)
  local copies, waits for them, and re-layouts  15.5 us (2%)
  between operations  14.8 us (2%)
  starting transfers between devices  10.5 us (1%)
    reduce_scatter x3, waiting for transfers between devices, row_sum(): return lax.psum_scatter(partial_value, 'o', scatter_dimension=0, tiled=True)  173 us
    pallas_call x3, Pallas kernels, token_gather(): pl.pallas_call(lambda *refs: gather_kernel(1, *refs), in_specs=[pl.BlockS...  121 us
    pallas_call x2, Pallas kernels, product_sum(): pl.pallas_call(kernel, in_specs=[pl.BlockSpec(memory_space=pl.ANY)] * cou...  102 us
    pallas_call x1, Pallas kernels, closing(): pl.pallas_call(kernel, in_specs=[hbm] * count + [vmem] * 2, out_specs=[vm...  55.6 us
    pallas_call x3, Pallas kernels, weight_grads(): pl.pallas_call(kernel, grid=(width // tile,), in_specs=specs, out_specs=p...  54.4 us
    pallas_call x1, Pallas kernels, input_gradient(): pl.pallas_call(kernel, in_specs=[hbm] * count + [vmem] * 3, out_specs=[vm...  52.1 us
    pallas_call x1, Pallas kernels, opening_gather(): pl.pallas_call(lambda *refs: opening_kernel(outer, *refs), in_specs=[vmem...  49.6 us
    ppermute x3, waiting for transfers between devices, exchange_rows(): other = lax.ppermute(jnp.where(side == 0, high, low), 'i', swap)  45.4 us
  transfers between devices with their start and end apart: 12, of which 8 were waited for; matrix products, arithmetic and copies ran while one was open for 6% of the time, Pallas kernels for 38%

profile of v1, /device:TPU:0, one launch (start us, length us, event | category | flops | bytes accessed | tf_op | source)
XLA Modules:
  0.0 877.5 jit_solution(14766598412988338714)
XLA Ops:
  12.7 11.9 %collective-permute-done = bf16[256,1024]{1,0:T(8,128)(2,1)S(1)} collective-permute-done((bf16[256,1024]{1,0:T(8,128)(2,1)S(1)}, bf16[256,1024]{1,0:T(8,128)(2,1)S(1)}, u32[]{:S(2)}, u32[]{:S(2)}) %collective-permute-start) | collective-permute-done | bytes 524320 | tf_op jit(solution)/shard_map/ppermute | solution.py:730
  30.6 17.0 %collective-permute-done.1 = bf16[256,1536]{1,0:T(8,128)(2,1)S(1)} collective-permute-done((bf16[256,1536]{1,0:T(8,128)(2,1)S(1)}, bf16[256,1536]{1,0:T(8,128)(2,1)S(1)}, u32[]{:S(2)}, u32[]{:S(2)}) %collective-permute-start.1) | collective-permute-done | bytes 786464 | tf_op jit(solution)/shard_map/ppermute | solution.py:730
  51.0 16.5 %collective-permute-done.2 = bf16[256,1536]{1,0:T(8,128)(2,1)S(1)} collective-permute-done((bf16[256,1536]{1,0:T(8,128)(2,1)S(1)}, bf16[256,1536]{1,0:T(8,128)(2,1)S(1)}, u32[]{:S(2)}, u32[]{:S(2)}) %collective-permute-start.2) | collective-permute-done | bytes 786464 | tf_op jit(solution)/shard_map/ppermute | solution.py:730
  69.8 49.6 %opening_gather.1 = (bf16[2048,2048]{1,0:T(8,128)(2,1)}, bf16[8,16,256]{2,1,0:T(8,128)(2,1)}) custom-call(bf16[256,2048]{1,0:T(8,128)(2,1)} %refs_6_.1, bf16[16,256]{1,0:T(8,128)(2,1)} %fusion.9.refs_1_), custom_call_target="tpu_custom_call" | custom-call | bytes 104857600 | tf_op jit(solution)/shard_map/opening_gather/pallas_call | solution.py:146
  128.8 8.6 fusion.2.refs_0_
  137.4 40.0 %token_gather.4.cotangent_ref.refs_2_ = bf16[2048,2048]{1,0:T(8,128)(2,1)} custom-call(bf16[256,2048]{1,0:T(8,128)(2,1)} %refs_0_.2), custom_call_target="tpu_custom_call" | custom-call | bytes 104857600 | tf_op jit(solution)/shard_map/token_gather/pallas_call | solution.py:171
  177.5 11.7 %fusion.3.query_ref.key_ref.value_ref = f32[2048,768]{1,0:T(8,128)} fusion(bf16[2048,2048]{1,0:T(8,128)(2,1)} %fusion.2.refs_0_, bf16[2048,1024]{1,0:T(8,128)(2,1)} %all-gather.4.cloned.1.call-done.refs_1_.refs_3_.refs_4_.refs_5_), kind=kOutput, calls=%fused_computation.5 | convolution fusion | flops 6442450944 | bytes 17825792 | tf_op jit(solution)/shard_map/dot_general | solution.py:21
  189.2 16.4 %attention_forward.1 = (bf16[2048,256]{1,0:T(8,128)(2,1)}, bf16[2048,256]{1,0:T(8,128)(2,1)}, bf16[2048,256]{1,0:T(8,128)(2,1)}, bf16[2048,256]{1,0:T(8,128)(2,1)}) custom-call(f32[2048,768]{1,0:T(8,128)} %fusion.3.query_ref.key_ref.value_ref, f32[2048,768]{1,0:T(8,128)} %fusion.3.query_ref.key_ref.value_ref, f32[2048,768]{1,0:T(8,128)} %fusion.3.query_ref.key_ref.value_ref, ...), custom_call_target="tpu_custom_call" | custom-call | flops 2147483648 | bytes 8388608 | tf_op jit(solution)/shard_map/attention_forward/pallas_call | solution.py:620
  205.6 44.2 %shard_map.194 = f32[256,2048]{1,0:T(8,128)} custom-call(bf16[2048,256]{1,0:T(8,128)(2,1)} %get-tuple-element.41.refs_0_.refs_5_, bf16[2048,1024]{1,0:T(8,128)(2,1)} %all-gather.4.cloned.1.call-done.refs_1_.refs_3_.refs_4_.refs_5_), custom_call_target="tpu_custom_call" | custom-call | flops 2147483648 | bytes 52428800 | tf_op jit(solution)/shard_map/pallas_call | solution.py:387
  253.3 40.2 %token_gather.3.normed_ref.refs_0_ = bf16[2048,2048]{1,0:T(8,128)(2,1)} custom-call(bf16[256,2048]{1,0:T(8,128)(2,1)} %multiply_convert_fusion.refs_0_), custom_call_target="tpu_custom_call" | custom-call | bytes 104857600 | tf_op jit(solution)/shard_map/token_gather/pallas_call | solution.py:171
  293.5 19.2 %feed_units.2.refs_1_.refs_3_.refs_0_ = bf16[2048,1536]{1,0:T(8,128)(2,1)} custom-call(bf16[2048,2048]{1,0:T(8,128)(2,1)} %token_gather.3.normed_ref.refs_0_, bf16[2048,2048]{1,0:T(8,128)(2,1)} %token_gather.4.cotangent_ref.refs_2_, bf16[2048,1536]{1,0:T(8,128)(2,1)} %all-gather.6.cloned.1.call-done.weight_ref.refs_2_), custom_call_target="tpu_custom_call" | custom-call | flops 12884901888 | bytes 29360128 | tf_op jit(solution)/shard_map/feed_units/pallas_call | solution.py:665
  312.7 19.6 %shard_map.195 = bf16[2048,1536]{1,0:T(8,128)(2,1)} custom-call(bf16[2048,2048]{1,0:T(8,128)(2,1)} %token_gather.3.normed_ref.refs_0_, bf16[2048,1536]{1,0:T(8,128)(2,1)} %feed_units.2.refs_1_.refs_3_.refs_0_, bf16[2048,2048]{1,0:T(8,128)(2,1)} %token_gather.4.cotangent_ref.refs_2_, bf16[2048,1536]{1,0:T(8,128)(2,1)} %feed_units.2.refs_1_.refs_3_.refs_0_), custom_call_target="tpu_custom_call" | custom-call | flops 12884901888 | bytes 29360128 | tf_op jit(solution)/shard_map/pallas_call | solution.py:707
  340.0 19.2 %feed_units.3.refs_1_.refs_3_ = bf16[2048,1536]{1,0:T(8,128)(2,1)} custom-call(bf16[2048,2048]{1,0:T(8,128)(2,1)} %token_gather.3.normed_ref.refs_0_, bf16[2048,2048]{1,0:T(8,128)(2,1)} %token_gather.4.cotangent_ref.refs_2_, bf16[2048,1536]{1,0:T(8,128)(2,1)} %all-gather.8.cloned.1.call-done.weight_ref.refs_3_), custom_call_target="tpu_custom_call" | custom-call | flops 12884901888 | bytes 29360128 | tf_op jit(solution)/shard_map/feed_units/pallas_call | solution.py:665
  359.2 19.1 %shard_map.196 = bf16[2048,1536]{1,0:T(8,128)(2,1)} custom-call(bf16[2048,2048]{1,0:T(8,128)(2,1)} %token_gather.3.normed_ref.refs_0_, bf16[2048,1536]{1,0:T(8,128)(2,1)} %feed_units.3.refs_1_.refs_3_, bf16[2048,2048]{1,0:T(8,128)(2,1)} %token_gather.4.cotangent_ref.refs_2_, bf16[2048,1536]{1,0:T(8,128)(2,1)} %feed_units.3.refs_1_.refs_3_), custom_call_target="tpu_custom_call" | custom-call | flops 12884901888 | bytes 29360128 | tf_op jit(solution)/shard_map/pallas_call | solution.py:707
  378.3 58.2 %shard_map.197 = f32[256,2048]{1,0:T(8,128)} custom-call(bf16[2048,1536]{1,0:T(8,128)(2,1)} %feed_units.2.refs_1_.refs_3_.refs_0_, bf16[2048,1536]{1,0:T(8,128)(2,1)} %feed_units.3.refs_1_.refs_3_, bf16[2048,1536]{1,0:T(8,128)(2,1)} %all-gather.6.cloned.1.call-done.weight_ref.refs_2_, bf16[2048,1536]{1,0:T(8,128)(2,1)} %all-gather.8.cloned.1.call-done.weight_ref.refs_3_), custom_call_target="tpu_custom_call" | custom-call | flops 17179869184 | bytes 52428800 | tf_op jit(solution)/shard_map/pallas_call | solution.py:387
  441.3 40.4 %token_gather.5.refs_4_ = bf16[2048,2048]{1,0:T(8,128)(2,1)} custom-call(bf16[256,2048]{1,0:T(8,128)(2,1)} %get-tuple-element.63.refs_0_), custom_call_target="tpu_custom_call" | custom-call | bytes 104857600 | tf_op jit(solution)/shard_map/token_gather/pallas_call | solution.py:171
  488.6 30.5 %attention_backward.1 = (bf16[2048,256]{1,0:T(8,128)(2,1)}, bf16[2048,256]{1,0:T(8,128)(2,1)}, bf16[2048,256]{1,0:T(8,128)(2,1)}) custom-call(bf16[2048,256]{1,0:T(8,128)(2,1)} %get-tuple-element.47.query_ref, bf16[2048,256]{1,0:T(8,128)(2,1)} %get-tuple-element.48.key_ref, bf16[2048,256]{1,0:T(8,128)(2,1)} %get-tuple-element.49.value_ref, ...), custom_call_target="tpu_custom_call" | custom-call | flops 5368709120 | bytes 8388608 | tf_op jit(solution)/shard_map/attention_backward/pallas_call | solution.py:635
  519.1 15.6 %shard_map.198 = bf16[2048,1024]{1,0:T(8,128)(2,1)} custom-call(bf16[2048,2048]{1,0:T(8,128)(2,1)} %fusion.2.refs_0_, bf16[2048,256]{1,0:T(8,128)(2,1)} %get-tuple-element.53.refs_1_.refs_0_, bf16[2048,256]{1,0:T(8,128)(2,1)} %get-tuple-element.51.refs_2_.refs_1_, bf16[2048,256]{1,0:T(8,128)(2,1)} %get-tuple-element.52.refs_3_.refs_2_, ...), custom_call_target="tpu_custom_call" | custom-call | flops 8589934592 | bytes 25165824 | tf_op jit(solution)/shard_map/pallas_call | solution.py:707
  536.0 52.1 %input_gradient.1 = (f32[256,2048]{1,0:T(8,128)}, f32[1,2048]{1,0:T(1,128)}) custom-call(bf16[2048,256]{1,0:T(8,128)(2,1)} %get-tuple-element.53.refs_1_.refs_0_, bf16[2048,256]{1,0:T(8,128)(2,1)} %get-tuple-element.51.refs_2_.refs_1_, bf16[2048,256]{1,0:T(8,128)(2,1)} %get-tuple-element.52.refs_3_.refs_2_, ...), custom_call_target="tpu_custom_call" | custom-call | flops 6442450944 | bytes 78643200 | tf_op jit(solution)/shard_map/input_gradient/pallas_call | solution.py:430
  589.5 55.6 %closing.1 = (f32[256,2048]{1,0:T(8,128)}, f32[8,2048]{1,0:T(8,128)}) custom-call(bf16[2048,1536]{1,0:T(8,128)(2,1)} %feed_units.2.refs_1_.refs_3_.refs_0_, bf16[2048,1536]{1,0:T(8,128)(2,1)} %feed_units.3.refs_1_.refs_3_, bf16[2048,1536]{1,0:T(8,128)(2,1)} %all-gather.6.cloned.1.call-done.weight_ref.refs_2_, ...), custom_call_target="tpu_custom_call" | custom-call | flops 8589934592 | bytes 78643200 | tf_op jit(solution)/shard_map/closing/pallas_call | solution.py:498
  649.2 10.7 %collective-permute-done.3 = bf16[256,1024]{1,0:T(8,128)(2,1)S(1)} collective-permute-done((bf16[256,1024]{1,0:T(8,128)(2,1)S(1)}, bf16[256,1024]{1,0:T(8,128)(2,1)S(1)}, u32[]{:S(2)}, u32[]{:S(2)}) %collective-permute-start.3) | collective-permute-done | bytes 524320 | tf_op jit(solution)/shard_map/ppermute | solution.py:748
  661.3 65.6 %reduce-scatter.6.cloned.1.call-done = bf16[512,1536]{1,0:T(8,128)(2,1)} async-done(((bf16[2048,1536]{1,0:T(8,128)(2,1)}), bf16[512,1536]{1,0:T(8,128)(2,1)}) %reduce-scatter.6.cloned.1.call-update) | async-done | bytes 1572880 | tf_op jit(solution)/shard_map/reduce_scatter | solution.py:741
  733.1 107.2 %reduce-scatter.8.cloned.1.call-done = bf16[512,1536]{1,0:T(8,128)(2,1)} async-done(((bf16[2048,1536]{1,0:T(8,128)(2,1)}), bf16[512,1536]{1,0:T(8,128)(2,1)}) %reduce-scatter.8.cloned.1.call-update) | async-done | bytes 1572880 | tf_op jit(solution)/shard_map/reduce_scatter | solution.py:741
  843.5 17.3 %collective-permute-done.5 = bf16[256,1536]{1,0:T(8,128)(2,1)S(1)} collective-permute-done((bf16[256,1536]{1,0:T(8,128)(2,1)S(1)}, bf16[256,1536]{1,0:T(8,128)(2,1)S(1)}, u32[]{:S(2)}, u32[]{:S(2)}) %collective-permute-start.5) | collective-permute-done | bytes 786464 | tf_op jit(solution)/shard_map/ppermute | solution.py:748
  (104 shorter events, 76.2 us)
Async XLA Ops:
  7.2 170.3 %all-gather.4.cloned.1.call-start = ((), (), s32[]{:S(2)}) async-start(), calls=%async_computation.3 | async-start | bytes 5242880 | tf_op jit(solution)/shard_map/all_gather | solution.py:737
  9.6 15.0 %collective-permute-start = (bf16[256,1024]{1,0:T(8,128)(2,1)S(1)}, bf16[256,1024]{1,0:T(8,128)(2,1)S(1)}, u32[]{:S(2)}, u32[]{:S(2)}) collective-permute-start(bf16[256,1024]{1,0:T(8,128)(2,1)S(1)} %broadcast_select_fusion.16), channel_id=1, source_target_pairs={{0,4},{4,0},{1,5},{5,1},{2,6},{6,2},{3,7},{7,3},{8,12},{12,8},{9,1... | collective-permute-start | bytes 1572872 | tf_op jit(solution)/shard_map/ppermute | solution.py:730
  24.9 1.6 copy-start.8
  25.9 267.5 %all-gather.6.cloned.1.call-start = ((), (), s32[]{:S(2)}) async-start(), calls=%async_computation.4 | async-start | bytes 7864320 | tf_op jit(solution)/shard_map/all_gather | solution.py:737
  28.8 18.8 %collective-permute-start.1 = (bf16[256,1536]{1,0:T(8,128)(2,1)S(1)}, bf16[256,1536]{1,0:T(8,128)(2,1)S(1)}, u32[]{:S(2)}, u32[]{:S(2)}) collective-permute-start(bf16[256,1536]{1,0:T(8,128)(2,1)S(1)} %broadcast_select_fusion.10), channel_id=1, source_target_pairs={{0,4},{4,0},{1,5},{5,1},{2,6},{6,2},{3,7},{7,3},{8,12},{12,8},{9,1... | collective-permute-start | bytes 2359304 | tf_op jit(solution)/shard_map/ppermute | solution.py:730
  49.2 290.8 %all-gather.8.cloned.1.call-start = ((), (), s32[]{:S(2)}) async-start(), calls=%async_computation.5 | async-start | bytes 7864320 | tf_op jit(solution)/shard_map/all_gather | solution.py:737
  49.5 18.0 %collective-permute-start.2 = (bf16[256,1536]{1,0:T(8,128)(2,1)S(1)}, bf16[256,1536]{1,0:T(8,128)(2,1)S(1)}, u32[]{:S(2)}, u32[]{:S(2)}) collective-permute-start(bf16[256,1536]{1,0:T(8,128)(2,1)S(1)} %broadcast_select_fusion.6), channel_id=1, source_target_pairs={{0,4},{4,0},{1,5},{5,1},{2,6},{6,2},{3,7},{7,3},{8,12},{12,8},{9,1... | collective-permute-start | bytes 2359304 | tf_op jit(solution)/shard_map/ppermute | solution.py:730
  67.9 1.3 copy-start.11
  67.9 1.4 copy-start.12
  69.1 576.0 %reduce-scatter.4.cloned.1.call-start = ((), (), s32[]{:S(2)}) async-start(), calls=%async_computation.6 | async-start | bytes 5242880 | tf_op jit(solution)/shard_map/reduce_scatter | solution.py:741
  125.7 11.7 %copy-start.10 = (f32[8,1,256]{2,1,0:T(1,128)}, f32[8,1,256]{2,1,0:T(1,128)S(1)}, u32[]{:S(2)}) copy-start(f32[8,1,256]{2,1,0:T(1,128)S(1)} %get-tuple-element.122) | copy-start | bytes 24580
  205.6 44.2 %copy-start.2 = (bf16[256,2048]{1,0:T(8,128)(2,1)S(1)}, bf16[256,2048]{1,0:T(8,128)(2,1)}, u32[]{:S(2)}) copy-start(bf16[256,2048]{1,0:T(8,128)(2,1)} %refs_6_.1) | copy-start | bytes 3145732
  251.8 187.1 %copy-start = (f32[256,2048]{1,0:T(8,128)}, f32[256,2048]{1,0:T(8,128)S(1)}, u32[]{:S(2)}) copy-start(f32[256,2048]{1,0:T(8,128)S(1)} %get-tuple-element.66.refs_4_) | copy-start | bytes 6291460
  436.5 2.4 copy-start.1
  436.6 2.5 copy-start.3
  534.7 192.2 %reduce-scatter.6.cloned.1.call-start = ((), (), s32[]{:S(2)}) async-start(), calls=%async_computation.7 | async-start | bytes 7864320 | tf_op jit(solution)/shard_map/reduce_scatter | solution.py:741
  535.3 305.0 %reduce-scatter.8.cloned.1.call-start = ((), (), s32[]{:S(2)}) async-start(), calls=%async_computation.8 | async-start | bytes 7864320 | tf_op jit(solution)/shard_map/reduce_scatter | solution.py:741
  646.3 13.6 %collective-permute-start.3 = (bf16[256,1024]{1,0:T(8,128)(2,1)S(1)}, bf16[256,1024]{1,0:T(8,128)(2,1)S(1)}, u32[]{:S(2)}, u32[]{:S(2)}) collective-permute-start(bf16[256,1024]{1,0:T(8,128)(2,1)S(1)} %constant_dynamic-slice_fusion.4), channel_id=1, source_target_pairs={{0,4},{4,0},{1,5},{5,1},{2,6},{6,2},{3,7},{7,3},{8,12},{12,8},{9,1... | collective-permute-start | bytes 1572872 | tf_op jit(solution)/shard_map/ppermute | solution.py:748
  728.1 114.9 %collective-permute-start.4 = (bf16[256,1536]{1,0:T(8,128)(2,1)S(1)}, bf16[256,1536]{1,0:T(8,128)(2,1)S(1)}, u32[]{:S(2)}, u32[]{:S(2)}) collective-permute-start(bf16[256,1536]{1,0:T(8,128)(2,1)S(1)} %constant_dynamic-slice_fusion.3), channel_id=1, source_target_pairs={{0,4},{4,0},{1,5},{5,1},{2,6},{6,2},{3,7},{7,3},{8,12},{12,8},{9,1... | collective-permute-start | bytes 2359304 | tf_op jit(solution)/shard_map/ppermute | solution.py:748
  730.5 112.5 %copy-start.7 = (bf16[512,1536]{1,0:T(8,128)(2,1)S(1)}, bf16[512,1536]{1,0:T(8,128)(2,1)}, u32[]{:S(2)}) copy-start(bf16[512,1536]{1,0:T(8,128)(2,1)} %reduce-scatter.6.cloned.1.call-done) | copy-start | bytes 4718596
  841.5 19.3 %collective-permute-start.5 = (bf16[256,1536]{1,0:T(8,128)(2,1)S(1)}, bf16[256,1536]{1,0:T(8,128)(2,1)S(1)}, u32[]{:S(2)}, u32[]{:S(2)}) collective-permute-start(bf16[256,1536]{1,0:T(8,128)(2,1)S(1)} %constant_dynamic-slice_fusion.2), channel_id=1, source_target_pairs={{0,4},{4,0},{1,5},{5,1},{2,6},{6,2},{3,7},{7,3},{8,12},{12,8},{9,1... | collective-permute-start | bytes 2359304 | tf_op jit(solution)/shard_map/ppermute | solution.py:748
  843.4 17.4 %copy-start.6 = (bf16[512,1536]{1,0:T(8,128)(2,1)S(1)}, bf16[512,1536]{1,0:T(8,128)(2,1)}, u32[]{:S(2)}) copy-start(bf16[512,1536]{1,0:T(8,128)(2,1)} %reduce-scatter.8.cloned.1.call-done) | copy-start | bytes 4718596
  864.4 2.3 copy-start.5
  866.7 2.3 copy-start.4
  (1 other events, 1.3 us)
Sparse Core Ops, SparseCore 0:
  26.1 82.2 all-gather.3
  110.5 113.8 all-gather.5
  226.5 113.5 all-gather.7
  534.8 74.3 reduce-scatter.3
  611.4 115.4 reduce-scatter.5
  729.1 111.2 reduce-scatter.7

commit v2 on v1

--- a/solution.py
+++ b/solution.py
@@ -9,7 +9,7 @@
 LEN = 1024
 BLK = 256
 PAIR = 2 * HD
-CHUNKS = 2
+EIGHTHS = (6, 2)
 
 epsilon = 1e-05
 rope_base = 130000.0
@@ -263,7 +263,7 @@
 
     def run(self, second_inside):
         width = self.total.shape[1]
-        tile = 512
+        tile = 1024
         for copy in self.right_copies():
             copy.wait()
 
@@ -397,14 +397,14 @@
     )(*sum_operands(terms))
 
 
-def input_gradient(terms, inputs, grad_hidden, gain):
+def input_gradient(terms, inputs, gain):
     rows, width = inputs.shape
     count = 2 * len(terms)
     tile = 32
 
     def kernel(*refs):
-        input_ref, grad_hidden_ref, gain_ref, grad_out, part_out = refs[count : count + 5]
-        steps = sum_steps(terms, refs[:count], grad_out, refs[count + 5 :])
+        input_ref, gain_ref, grad_out, part_out = refs[count : count + 4]
+        steps = sum_steps(terms, refs[:count], grad_out, refs[count + 4 :])
         steps.load()
         greet_partners()
         steps.run(True)
@@ -418,7 +418,7 @@
             grad_normed = grad_out[span, :]
             scaled = grad_normed * gain_ref[...]
             mean = jnp.mean(scaled * normed, axis=-1, keepdims=True)
-            grad_out[span, :] = grad_hidden_ref[span, :] + inverse * (scaled - normed * mean)
+            grad_out[span, :] = inverse * (scaled - normed * mean)
             return part + jnp.sum(grad_normed * normed, axis=0, keepdims=True)
 
         part_out[...] = lax.fori_loop(
@@ -429,7 +429,7 @@
     vmem, hbm = pl.BlockSpec(memory_space=pltpu.VMEM), pl.BlockSpec(memory_space=pl.ANY)
     return pl.pallas_call(
         kernel,
-        in_specs=[hbm] * count + [vmem] * 3,
+        in_specs=[hbm] * count + [vmem] * 2,
         out_specs=[vmem] * 2,
         out_shape=[
             jax.ShapeDtypeStruct((rows, width), jnp.float32),
@@ -441,16 +441,16 @@
             flops=sum_flops(terms), bytes_accessed=150 * rows * width, transcendentals=rows
         ),
         name="input_gradient",
-    )(*sum_operands(terms), inputs, grad_hidden, gain.reshape(1, width))
-
-
-def closing(terms, hidden, parts, outer):
-    rows, width = hidden.shape
+    )(*sum_operands(terms), inputs, gain.reshape(1, width))
+
+
+def closing(terms, parts, outer):
+    rows, width = terms[0][0].shape[0] // 8, terms[0][2].shape[0]
     count = 2 * len(terms)
 
     def kernel(*refs):
-        hidden_ref, part_ref, layer_out, total_out = refs[count : count + 4]
-        scratch = refs[count + 4 :]
+        part_ref, layer_out, total_out = refs[count : count + 3]
+        scratch = refs[count + 3 :]
         held, stages, semaphores, row_semaphores = scratch[-4:]
         output = sum_steps(terms, refs[:count], layer_out, scratch[:-4])
         output.load()
@@ -484,7 +484,6 @@
             started.append(copy)
         output.second()
         output.finish()
-        layer_out[...] += hidden_ref[...]
         value = stages[2]
         for shift in range(1, outer):
             started[2 + shift].wait_recv()
@@ -497,7 +496,7 @@
     vmem, hbm = pl.BlockSpec(memory_space=pltpu.VMEM), pl.BlockSpec(memory_space=pl.ANY)
     return pl.pallas_call(
         kernel,
-        in_specs=[hbm] * count + [vmem] * 2,
+        in_specs=[hbm] * count + [vmem],
         out_specs=[vmem] * 2,
         out_shape=[
             jax.ShapeDtypeStruct((rows, width), jnp.float32),
@@ -515,7 +514,7 @@
             flops=sum_flops(terms), bytes_accessed=150 * rows * width, transcendentals=0
         ),
         name="closing",
-    )(*sum_operands(terms), hidden, parts)
+    )(*sum_operands(terms), parts)
 
 
 def rope_tables():
@@ -644,6 +643,52 @@
     )(queries, keys, values, grads, *tables)
 
 
+def norm_kernel(input_ref, gain_ref, out_ref):
+    values = input_ref[...].astype(jnp.float32)
+    out_ref[...] = (values * inverse_rms(values) * gain_ref[...]).astype(jnp.bfloat16)
+
+
+def norm_rows(inputs, gain):
+    rows, width = inputs.shape
+    tile = 256
+    block = pl.BlockSpec((tile, width), lambda t: (t, 0))
+    return pl.pallas_call(
+        norm_kernel,
+        grid=(rows // tile,),
+        in_specs=[block, pl.BlockSpec((1, width), lambda t: (0, 0))],
+        out_specs=block,
+        out_shape=jax.ShapeDtypeStruct((rows, width), jnp.bfloat16),
+        cost_estimate=pl.CostEstimate(
+            flops=4 * rows * width, bytes_accessed=4 * rows * width, transcendentals=rows
+        ),
+        name="norm_rows",
+    )(inputs, gain.reshape(1, width))
+
+
+def product_kernel(left_ref, right_ref, out_ref):
+    out_ref[...] = contract(left_ref[...], right_ref[...], 1, 0).astype(out_ref.dtype)
+
+
+def product(left, right, start, columns, kind):
+    rows, width = left.shape
+    tile = 512
+    return pl.pallas_call(
+        product_kernel,
+        grid=(rows // tile,),
+        in_specs=[
+            pl.BlockSpec((tile, width), lambda t: (t, 0)),
+            pl.BlockSpec((width, columns), lambda t: (0, start // columns)),
+        ],
+        out_specs=pl.BlockSpec((tile, columns), lambda t: (t, 0)),
+        out_shape=jax.ShapeDtypeStruct((rows, columns), kind),
+        cost_estimate=pl.CostEstimate(
+            flops=2 * rows * width * columns,
+            bytes_accessed=2 * rows * width + 2 * width * columns + 4 * rows * columns,
+            transcendentals=0,
+        ),
+    )(left, right)
+
+
 def feed_kernel(normed_ref, cotangent_ref, weight_ref, out_ref):
     chunk = out_ref.shape[1] // 3
     gate, up, down = [slice(which * chunk, (which + 1) * chunk) for which in range(3)]
@@ -718,7 +763,7 @@
     )(*operands)
 
 
-def exchange_rows(weights, first, width):
+def own_and_other(weights, first, width):
     side = lax.axis_index("i")
 
     def columns(half):
@@ -727,10 +772,11 @@
 
     low, high = columns(0), columns(1)
     kept = jnp.where(side == 0, low, high)
-    other = lax.ppermute(jnp.where(side == 0, high, low), "i", swap)
-    return jnp.concatenate(
-        [jnp.where(side == 0, kept, other), jnp.where(side == 0, other, kept)]
-    )
+    return kept, lax.ppermute(jnp.where(side == 0, high, low), "i", swap)
+
+
+def exchange_rows(weights, first, width):
+    return jnp.concatenate(in_order(own_and_other(weights, first, width)))
 
 
 def row_gather(values):
@@ -776,29 +822,29 @@
 ):
     head_width = query_weight.shape[1] // 2
     hidden = gate_weight.shape[1] // 2
-    chunk = hidden // CHUNKS
+    chunks = [hidden * part // 8 for part in EIGHTHS]
+    firsts = [sum(chunks[:k]) for k in range(len(chunks))]
     tables = rope_tables()
     outer = lax.axis_size("o")
 
-    attention_rows = exchange_rows(
-        (query_weight, key_weight, value_weight, out_weight), 0, head_width
-    )
-    attention_full = row_gather(attention_rows)
+    kept, other = own_and_other((query_weight, key_weight, value_weight, out_weight), 0, head_width)
+    kept_full = row_gather(kept)
+    other_full = row_gather(other)
     feed_full = []
-    for k in range(CHUNKS):
-        feed_rows = exchange_rows((gate_weight, up_weight, down_weight), k * chunk, chunk)
+    for first, chunk in zip(firsts, chunks):
+        feed_rows = exchange_rows((gate_weight, up_weight, down_weight), first, chunk)
         feed_full.append(row_gather(feed_rows))
     inputs_all, gains = opening_gather(layer_input, jnp.stack([attention_gain, feed_gain]), outer)
     gain_one, gain_two = [g.astype(jnp.float32) for g in gains]
-    inputs_all = inputs_all.astype(jnp.float32)
-    normed = (inputs_all * inverse_rms(inputs_all) * gain_one).astype(jnp.bfloat16)
+    normed = norm_rows(inputs_all, gain_one)
     normed, tables, late = lax.optimization_barrier((normed, tables, out_cotangent))
     cotangents = token_gather(late)
     inputs = layer_input.astype(jnp.float32)
 
-    mixed = contract(normed, attention_full[:, : 3 * head_width], 1, 0)
+    blocks = [w.reshape(outer, *kept.shape) for w in (kept_full, other_full)]
+    attention_full = jnp.stack(in_order(blocks), axis=1).reshape(-1, kept.shape[1])
+    mixed = product(normed, attention_full, 0, 3 * head_width, jnp.float32)
     queries, keys, values, attended = attention_forward(mixed, tables)
-    out_full = attention_full[:, 3 * head_width :]
     hidden_state = inputs + product_sum(
         [(attended, 0, attention_full, 3 * head_width, head_width)], 3
     )
@@ -807,7 +853,7 @@
     normed_two = token_gather((normed_two_raw * gain_two).astype(jnp.bfloat16))
 
     output_terms, grad_terms, feed_grads = [], [], []
-    for k in range(CHUNKS):
+    for k, chunk in enumerate(chunks):
         units = feed_units(normed_two, cotangents, feed_full[k])
         grads = weight_grads(
             [
@@ -830,7 +876,7 @@
         scaled_two - normed_two_raw * jnp.mean(scaled_two * normed_two_raw, axis=-1, keepdims=True)
     )
     grad_rows = token_gather(grad_hidden.astype(jnp.bfloat16))
-    grad_attended = contract(grad_rows, out_full, 1, 0).astype(jnp.bfloat16)
+    grad_attended = product(grad_rows, attention_full, 3 * head_width, head_width, jnp.bfloat16)
     grad_query, grad_key, grad_value = attention_backward(
         queries, keys, values, grad_attended, tables
     )
@@ -843,32 +889,33 @@
     attention_grads, grad_query = lax.optimization_barrier((attention_grads, grad_query))
     attention_summed = row_sum(attention_grads)
     attention_halves = exchange_columns(attention_summed)
-    input_grad, attention_gain_part = input_gradient(
+    norm_grad, attention_gain_part = input_gradient(
         [
             (g, 0, attention_full, which * head_width, head_width)
             for which, g in enumerate((grad_query, grad_key, grad_value))
         ],
         layer_input,
-        grad_hidden,
         gain_one,
     )
     parts = jnp.concatenate([attention_gain_part, feed_gain_part, jnp.zeros((6, feed_gain_part.shape[1]))])
-    layer_output, gain_sums = closing(output_terms, hidden_state, parts, outer)
-
-    def whole_rows(halves, which, width):
+    feed_output, gain_sums = closing(output_terms, parts, outer)
+
+    def whole_rows(halves, which, widths):
         return jnp.concatenate(
             [
-                half[k][:, which * width : (which + 1) * width]
+                part[:, which * width : (which + 1) * width]
                 for half in zip(*halves)
-                for k in range(len(halves))
+                for part, width in zip(half, widths)
             ],
             axis=1,
         ).astype(jnp.float32)
 
+    input_grad = grad_hidden + norm_grad
+    layer_output = hidden_state + feed_output
     feed_halves = [in_order(halves) for halves in feed_grads]
-    feed_rows = [whole_rows(feed_halves, which, chunk) for which in range(3)]
+    feed_rows = [whole_rows(feed_halves, which, chunks) for which in range(3)]
     attention_halves = [in_order(attention_halves)]
-    attention_rows = [whole_rows(attention_halves, which, head_width) for which in range(4)]
+    attention_rows = [whole_rows(attention_halves, which, [head_width]) for which in range(4)]
     device = lax.axis_index("o")
     for axis in group:
         device = device * 2 + lax.axis_index(axis)

time: 884 us -> 812 us (0.919)
  waiting for transfers between devices: 255 us -> 185 us
  Pallas kernels: 520 us -> 548 us
  matrix products: 18.7 us -> 0 us
    reduce_scatter x3, waiting for transfers between devices: 173 us -> 117 us  [row_sum(): return lax.psum_scatter(partial_value, 'o', scatter_dimension=0, tiled=True)]
    pallas_call x2 -> x5, Pallas kernels: 108 us -> 131 us  [the longest x1 52.1 us: closing(): pl.pallas_call(kernel, in_specs=[hbm] * count + [vmem], out_specs=[vmem]...]
    dot_general x2 -> x0, matrix products: 18.7 us -> none  [contract(): lax.dot_general(left_side, right_side, (((left_dim,), (right_dim,)), ((),...]
  transfers between devices with their start and end apart: 12 -> 13, of which waited for: 8 -> 5; matrix products, arithmetic and copies ran while one was open for 6% -> 5% of each run, Pallas kernels for 38% -> 64%
where the time goes in v2:
time: 812 us; the launch traced here: 806 us
  Pallas kernels  548 us (67%)
  waiting for transfers between devices  185 us (23%)
  other arithmetic  39.3 us (5%)
  between operations  14.8 us (2%)
  starting transfers between devices  10.5 us (1%)
  local copies, waits for them, and re-layouts  8.92 us (1%)
    pallas_call x3, Pallas kernels, token_gather(): pl.pallas_call(lambda *refs: gather_kernel(1, *refs), in_specs=[pl.BlockS...  122 us
    reduce_scatter x3, waiting for transfers between devices, row_sum(): return lax.psum_scatter(partial_value, 'o', scatter_dimension=0, tiled=True)  117 us
    pallas_call x2, Pallas kernels, product_sum(): pl.pallas_call(kernel, in_specs=[pl.BlockSpec(memory_space=pl.ANY)] * cou...  98.4 us
    pallas_call x3, Pallas kernels, weight_grads(): pl.pallas_call(kernel, grid=(width // tile,), in_specs=specs, out_specs=p...  56.9 us
    pallas_call x1, Pallas kernels, opening_gather(): pl.pallas_call(lambda *refs: opening_kernel(outer, *refs), in_specs=[vmem...  52.2 us
    pallas_call x1, Pallas kernels, closing(): pl.pallas_call(kernel, in_specs=[hbm] * count + [vmem], out_specs=[vmem]...  52.1 us
    pallas_call x1, Pallas kernels, input_gradient(): pl.pallas_call(kernel, in_specs=[hbm] * count + [vmem] * 2, out_specs=[vm...  49.5 us
    pallas_call x2, Pallas kernels, feed_units(): pl.pallas_call(feed_kernel, grid=(rows // tile,), in_specs=[tokens, token...  40.9 us
  transfers between devices with their start and end apart: 13, of which 5 were waited for; matrix products, arithmetic and copies ran while one was open for 5% of the time, Pallas kernels for 64%

profile of v2, /device:TPU:0, one launch (start us, length us, event | category | flops | bytes accessed | tf_op | source)
XLA Modules:
  0.0 806.1 jit_solution(15743091509276519762)
XLA Ops:
  13.9 12.2 %collective-permute-done = bf16[256,1024]{1,0:T(8,128)(2,1)} collective-permute-done((bf16[256,1024]{1,0:T(8,128)(2,1)}, bf16[256,1024]{1,0:T(8,128)(2,1)}, u32[]{:S(2)}, u32[]{:S(2)}) %collective-permute-start) | collective-permute-done | bytes 524320 | tf_op jit(solution)/shard_map/ppermute | solution.py:775
  28.6 25.4 %collective-permute-done.1 = bf16[256,2304]{1,0:T(8,128)(2,1)S(1)} collective-permute-done((bf16[256,2304]{1,0:T(8,128)(2,1)S(1)}, bf16[256,2304]{1,0:T(8,128)(2,1)S(1)}, u32[]{:S(2)}, u32[]{:S(2)}) %collective-permute-start.1) | collective-permute-done | bytes 1179680 | tf_op jit(solution)/shard_map/ppermute | solution.py:775
  58.5 52.2 %opening_gather.1 = (bf16[2048,2048]{1,0:T(8,128)(2,1)}, bf16[8,16,256]{2,1,0:T(8,128)(2,1)}) custom-call(bf16[256,2048]{1,0:T(8,128)(2,1)} %refs_6_.1, bf16[16,256]{1,0:T(8,128)(2,1)} %fusion.3.refs_1_), custom_call_target="tpu_custom_call" | custom-call | bytes 104857600 | tf_op jit(solution)/shard_map/opening_gather/pallas_call | solution.py:146
  112.2 10.6 %norm_rows.1.left_ref.refs_0_ = bf16[2048,2048]{1,0:T(8,128)(2,1)} custom-call(bf16[2048,2048]{1,0:T(8,128)(2,1)} %get-tuple-element.36.input_ref, f32[1,2048]{1,0:T(1,128)} %convert.2.gain_ref.refs_7_), custom_call_target="tpu_custom_call" | custom-call | flops 16777216 | bytes 16777216 | tf_op jit(solution)/shard_map/norm_rows/pallas_call | solution.py:655
  125.6 40.8 %token_gather.4.cotangent_ref.refs_2_ = bf16[2048,2048]{1,0:T(8,128)(2,1)} custom-call(bf16[256,2048]{1,0:T(8,128)(2,1)} %refs_0_.2), custom_call_target="tpu_custom_call" | custom-call | bytes 104857600 | tf_op jit(solution)/shard_map/token_gather/pallas_call | solution.py:171
  172.6 11.8 %shard_map.194.query_ref.key_ref.value_ref = f32[2048,768]{1,0:T(8,128)} custom-call(bf16[2048,2048]{1,0:T(8,128)(2,1)} %norm_rows.1.left_ref.refs_0_, bf16[2048,1024]{1,0:T(8,128)(2,1)} %bitcast.15), custom_call_target="tpu_custom_call" | custom-call | flops 6442450944 | bytes 17825792 | tf_op jit(solution)/shard_map/pallas_call | solution.py:675
  184.5 16.4 %attention_forward.1 = (bf16[2048,256]{1,0:T(8,128)(2,1)}, bf16[2048,256]{1,0:T(8,128)(2,1)}, bf16[2048,256]{1,0:T(8,128)(2,1)}, bf16[2048,256]{1,0:T(8,128)(2,1)}) custom-call(f32[2048,768]{1,0:T(8,128)} %shard_map.194.query_ref.key_ref.value_ref, f32[2048,768]{1,0:T(8,128)} %shard_map.194.query_ref.key_ref.value_ref, ...), custom_call_target="tpu_custom_call" | custom-call | flops 2147483648 | bytes 8388608 | tf_op jit(solution)/shard_map/attention_forward/pallas_call | solution.py:619
  200.9 42.6 %shard_map.195 = f32[256,2048]{1,0:T(8,128)} custom-call(bf16[2048,256]{1,0:T(8,128)(2,1)} %get-tuple-element.41.refs_0_.refs_5_, bf16[2048,1024]{1,0:T(8,128)(2,1)} %bitcast.16), custom_call_target="tpu_custom_call" | custom-call | flops 2147483648 | bytes 52428800 | tf_op jit(solution)/shard_map/pallas_call | solution.py:387
  246.7 40.8 %token_gather.3.normed_ref.refs_0_ = bf16[2048,2048]{1,0:T(8,128)(2,1)} custom-call(bf16[256,2048]{1,0:T(8,128)(2,1)} %multiply_convert_fusion.refs_0_), custom_call_target="tpu_custom_call" | custom-call | bytes 104857600 | tf_op jit(solution)/shard_map/token_gather/pallas_call | solution.py:171
  287.5 27.1 %feed_units.2.refs_1_.refs_3_.refs_0_ = bf16[2048,2304]{1,0:T(8,128)(2,1)} custom-call(bf16[2048,2048]{1,0:T(8,128)(2,1)} %token_gather.3.normed_ref.refs_0_, bf16[2048,2048]{1,0:T(8,128)(2,1)} %token_gather.4.cotangent_ref.refs_2_, bf16[2048,2304]{1,0:T(8,128)(2,1)} %all-gather.9.cloned.1.call-done.weight_ref.refs_2_), custom_call_target="tpu_custom_call" | custom-call | flops 19327352832 | bytes 35651584 | tf_op jit(solution)/shard_map/feed_units/pallas_call | solution.py:710
  314.6 26.9 %shard_map.196 = bf16[2048,2304]{1,0:T(8,128)(2,1)} custom-call(bf16[2048,2048]{1,0:T(8,128)(2,1)} %token_gather.3.normed_ref.refs_0_, bf16[2048,2304]{1,0:T(8,128)(2,1)} %feed_units.2.refs_1_.refs_3_.refs_0_, bf16[2048,2048]{1,0:T(8,128)(2,1)} %token_gather.4.cotangent_ref.refs_2_, bf16[2048,2304]{1,0:T(8,128)(2,1)} %feed_units.2.refs_1_.refs_3_.refs_0_), custom_call_target="tpu_custom_call" | custom-call | flops 19327352832 | bytes 35651584 | tf_op jit(solution)/shard_map/pallas_call | solution.py:752
  341.5 13.8 %feed_units.3.refs_1_.refs_3_ = bf16[2048,768]{1,0:T(8,128)(2,1)} custom-call(bf16[2048,2048]{1,0:T(8,128)(2,1)} %token_gather.3.normed_ref.refs_0_, bf16[2048,2048]{1,0:T(8,128)(2,1)} %token_gather.4.cotangent_ref.refs_2_, bf16[2048,768]{1,0:T(8,128)(2,1)} %all-gather.11.cloned.1.call-done.weight_ref.refs_3_), custom_call_target="tpu_custom_call" | custom-call | flops 6442450944 | bytes 23068672 | tf_op jit(solution)/shard_map/feed_units/pallas_call | solution.py:710
  355.3 14.2 %shard_map.197 = bf16[2048,768]{1,0:T(8,128)(2,1)} custom-call(bf16[2048,2048]{1,0:T(8,128)(2,1)} %token_gather.3.normed_ref.refs_0_, bf16[2048,768]{1,0:T(8,128)(2,1)} %feed_units.3.refs_1_.refs_3_, bf16[2048,2048]{1,0:T(8,128)(2,1)} %token_gather.4.cotangent_ref.refs_2_, bf16[2048,768]{1,0:T(8,128)(2,1)} %feed_units.3.refs_1_.refs_3_), custom_call_target="tpu_custom_call" | custom-call | flops 6442450944 | bytes 23068672 | tf_op jit(solution)/shard_map/pallas_call | solution.py:752
  369.6 55.8 %shard_map.198 = f32[256,2048]{1,0:T(8,128)} custom-call(bf16[2048,2304]{1,0:T(8,128)(2,1)} %feed_units.2.refs_1_.refs_3_.refs_0_, bf16[2048,768]{1,0:T(8,128)(2,1)} %feed_units.3.refs_1_.refs_3_, bf16[2048,2304]{1,0:T(8,128)(2,1)} %all-gather.9.cloned.1.call-done.weight_ref.refs_2_, bf16[2048,768]{1,0:T(8,128)(2,1)} %all-gather.11.cloned.1.call-done.weight_ref.refs_3_), custom_call_target="tpu_custom_call" | custom-call | flops 17179869184 | bytes 52428800 | tf_op jit(solution)/shard_map/pallas_call | solution.py:387
  429.6 40.4 %token_gather.5.left_ref.refs_4_ = bf16[2048,2048]{1,0:T(8,128)(2,1)} custom-call(bf16[256,2048]{1,0:T(8,128)(2,1)} %fusion.11.refs_0_), custom_call_target="tpu_custom_call" | custom-call | bytes 104857600 | tf_op jit(solution)/shard_map/token_gather/pallas_call | solution.py:171
  469.9 6.6 shard_map.199.grad_ref
  476.5 30.3 %attention_backward.1 = (bf16[2048,256]{1,0:T(8,128)(2,1)}, bf16[2048,256]{1,0:T(8,128)(2,1)}, bf16[2048,256]{1,0:T(8,128)(2,1)}) custom-call(bf16[2048,256]{1,0:T(8,128)(2,1)} %get-tuple-element.47.query_ref, bf16[2048,256]{1,0:T(8,128)(2,1)} %get-tuple-element.48.key_ref, bf16[2048,256]{1,0:T(8,128)(2,1)} %get-tuple-element.49.value_ref, ...), custom_call_target="tpu_custom_call" | custom-call | flops 5368709120 | bytes 8388608 | tf_op jit(solution)/shard_map/attention_backward/pallas_call | solution.py:634
  506.8 15.8 %shard_map.200 = bf16[2048,1024]{1,0:T(8,128)(2,1)} custom-call(bf16[2048,2048]{1,0:T(8,128)(2,1)} %norm_rows.1.left_ref.refs_0_, bf16[2048,256]{1,0:T(8,128)(2,1)} %get-tuple-element.53.refs_1_.refs_0_, bf16[2048,256]{1,0:T(8,128)(2,1)} %get-tuple-element.51.refs_2_.refs_1_, bf16[2048,256]{1,0:T(8,128)(2,1)} %get-tuple-element.52.refs_3_.refs_2_, ...), custom_call_target="tpu_custom_call" | custom-call | flops 8589934592 | bytes 25165824 | tf_op jit(solution)/shard_map/pallas_call | solution.py:752
  523.5 49.5 %input_gradient.1 = (f32[256,2048]{1,0:T(8,128)}, f32[1,2048]{1,0:T(1,128)}) custom-call(bf16[2048,256]{1,0:T(8,128)(2,1)} %get-tuple-element.53.refs_1_.refs_0_, bf16[2048,256]{1,0:T(8,128)(2,1)} %get-tuple-element.51.refs_2_.refs_1_, bf16[2048,256]{1,0:T(8,128)(2,1)} %get-tuple-element.52.refs_3_.refs_2_, bf16[2048,1024]{1,0:T(8,128)(2,1)} %bitcast.18, ...), custom_call_target="tpu_custom_call" | custom-call | flops 6442450944 | bytes 78643200 | tf_op jit(solution)/shard_map/input_gradient/pallas_call | solution.py:430
  574.4 52.1 %closing.1 = (f32[256,2048]{1,0:T(8,128)}, f32[8,2048]{1,0:T(8,128)}) custom-call(bf16[2048,2304]{1,0:T(8,128)(2,1)} %feed_units.2.refs_1_.refs_3_.refs_0_, bf16[2048,768]{1,0:T(8,128)(2,1)} %feed_units.3.refs_1_.refs_3_, bf16[2048,2304]{1,0:T(8,128)(2,1)} %all-gather.9.cloned.1.call-done.weight_ref.refs_2_, ...), custom_call_target="tpu_custom_call" | custom-call | flops 8589934592 | bytes 78643200 | tf_op jit(solution)/shard_map/closing/pallas_call | solution.py:497
  626.5 6.2 fusion.10
  636.9 7.5 collective-permute-done.5
  648.0 117.0 %reduce-scatter.6.cloned.1.call-done = bf16[512,2304]{1,0:T(8,128)(2,1)} async-done(((bf16[2048,2304]{1,0:T(8,128)(2,1)}), bf16[512,2304]{1,0:T(8,128)(2,1)}) %reduce-scatter.6.cloned.1.call-update) | async-done | bytes 2359312 | tf_op jit(solution)/shard_map/reduce_scatter | solution.py:787
  771.7 22.0 %collective-permute-done.4 = bf16[256,2304]{1,0:T(8,128)(2,1)S(1)} collective-permute-done((bf16[256,2304]{1,0:T(8,128)(2,1)S(1)}, bf16[256,2304]{1,0:T(8,128)(2,1)S(1)}, u32[]{:S(2)}, u32[]{:S(2)}) %collective-permute-start.4) | collective-permute-done | bytes 1179680 | tf_op jit(solution)/shard_map/ppermute | solution.py:794
  (101 shorter events, 53.4 us)
Async XLA Ops:
  7.2 160.5 %all-gather.5.cloned.1.call-start = ((), (), s32[]{:S(2)}) async-start(), calls=%async_computation.3 | async-start | bytes 2621440 | tf_op jit(solution)/shard_map/all_gather | solution.py:783
  8.4 17.9 %copy-start.4 = (bf16[256,2048]{1,0:T(8,128)(2,1)S(1)}, bf16[256,2048]{1,0:T(8,128)(2,1)}, u32[]{:S(2)}) copy-start(bf16[256,2048]{1,0:T(8,128)(2,1)} %param.18) | copy-start | bytes 3145732
  9.6 16.7 %copy-start.5 = (bf16[256,2048]{1,0:T(8,128)(2,1)S(1)}, bf16[256,2048]{1,0:T(8,128)(2,1)}, u32[]{:S(2)}) copy-start(bf16[256,2048]{1,0:T(8,128)(2,1)} %param.16) | copy-start | bytes 3145732
  9.6 16.7 %copy-start.6 = (bf16[256,2048]{1,0:T(8,128)(2,1)S(1)}, bf16[256,2048]{1,0:T(8,128)(2,1)}, u32[]{:S(2)}) copy-start(bf16[256,2048]{1,0:T(8,128)(2,1)} %param.17) | copy-start | bytes 3145732
  10.9 156.8 %all-gather.7.cloned.1.call-start = ((), (), s32[]{:S(2)}) async-start(), calls=%async_computation.4 | async-start | bytes 2621440 | tf_op jit(solution)/shard_map/all_gather | solution.py:783
  10.9 15.3 %collective-permute-start = (bf16[256,1024]{1,0:T(8,128)(2,1)}, bf16[256,1024]{1,0:T(8,128)(2,1)}, u32[]{:S(2)}, u32[]{:S(2)}) collective-permute-start(bf16[256,1024]{1,0:T(8,128)(2,1)} %get-tuple-element.98), channel_id=1, source_target_pairs={{0,4},{4,0},{1,5},{5,1},{2,6},{6,2},{3,7},{7,3},{8,12},{12,8},{9,1... | collective-permute-start | bytes 1572872 | tf_op jit(solution)/shard_map/ppermute | solution.py:775
  26.2 261.3 %all-gather.9.cloned.1.call-start = ((), (), s32[]{:S(2)}) async-start(), calls=%async_computation.5 | async-start | bytes 11796480 | tf_op jit(solution)/shard_map/all_gather | solution.py:783
  26.8 27.2 %collective-permute-start.1 = (bf16[256,2304]{1,0:T(8,128)(2,1)S(1)}, bf16[256,2304]{1,0:T(8,128)(2,1)S(1)}, u32[]{:S(2)}, u32[]{:S(2)}) collective-permute-start(bf16[256,2304]{1,0:T(8,128)(2,1)S(1)} %broadcast_select_fusion.6), channel_id=1, source_target_pairs={{0,4},{4,0},{1,5},{5,1},{2,6},{6,2},{3,7},{7,3},{8,12},{12,8},{9,1... | collective-permute-start | bytes 3538952 | tf_op jit(solution)/shard_map/ppermute | solution.py:775
  56.1 1.8 copy-start.8
  56.1 1.8 copy-start.9
  56.1 285.4 %all-gather.11.cloned.1.call-start = ((), (), s32[]{:S(2)}) async-start(), calls=%async_computation.6 | async-start | bytes 3932160 | tf_op jit(solution)/shard_map/all_gather | solution.py:783
  56.4 110.0 %collective-permute-start.2 = (bf16[256,768]{1,0:T(8,128)(2,1)S(1)}, bf16[256,768]{1,0:T(8,128)(2,1)S(1)}, u32[]{:S(2)}, u32[]{:S(2)}) collective-permute-start(bf16[256,768]{1,0:T(8,128)(2,1)S(1)} %broadcast_select_fusion.16), channel_id=1, source_target_pairs={{0,4},{4,0},{1,5},{5,1},{2,6},{6,2},{3,7},{7,3},{8,12},{12,8},{9,1... | collective-permute-start | bytes 1179656 | tf_op jit(solution)/shard_map/ppermute | solution.py:775
  167.6 465.0 %reduce-scatter.8.cloned.1.call-start = ((), (), s32[]{:S(2)}) async-start(), calls=%async_computation.9 | async-start | bytes 3932160 | tf_op jit(solution)/shard_map/reduce_scatter | solution.py:787
  200.9 42.6 %copy-start.2 = (bf16[256,2048]{1,0:T(8,128)(2,1)S(1)}, bf16[256,2048]{1,0:T(8,128)(2,1)}, u32[]{:S(2)}) copy-start(bf16[256,2048]{1,0:T(8,128)(2,1)} %refs_6_.1) | copy-start | bytes 3145732
  369.5 276.0 %reduce-scatter.4.cloned.1.call-start = ((), (), s32[]{:S(2)}) async-start(), calls=%async_computation.7 | async-start | bytes 5242880 | tf_op jit(solution)/shard_map/reduce_scatter | solution.py:787
  425.4 2.4 copy-start
  425.4 2.5 copy-start.1
  522.6 242.3 %reduce-scatter.6.cloned.1.call-start = ((), (), s32[]{:S(2)}) async-start(), calls=%async_computation.8 | async-start | bytes 11796480 | tf_op jit(solution)/shard_map/reduce_scatter | solution.py:787
  633.7 10.7 %collective-permute-start.5 = (bf16[256,768]{1,0:T(8,128)(2,1)S(1)}, bf16[256,768]{1,0:T(8,128)(2,1)S(1)}, u32[]{:S(2)}, u32[]{:S(2)}) collective-permute-start(bf16[256,768]{1,0:T(8,128)(2,1)S(1)} %constant_dynamic-slice_fusion.2), channel_id=1, source_target_pairs={{0,4},{4,0},{1,5},{5,1},{2,6},{6,2},{3,7},{7,3},{8,12},{12,8},{9,1... | collective-permute-start | bytes 1179656 | tf_op jit(solution)/shard_map/ppermute | solution.py:794
  645.6 122.3 %copy-start.7 = (bf16[512,1024]{1,0:T(8,128)(2,1)S(1)}, bf16[512,1024]{1,0:T(8,128)(2,1)}, u32[]{:S(2)}) copy-start(bf16[512,1024]{1,0:T(8,128)(2,1)} %reduce-scatter.4.cloned.1.call-done) | copy-start | bytes 3145732
  646.8 121.1 %collective-permute-start.3 = (bf16[256,1024]{1,0:T(8,128)(2,1)S(1)}, bf16[256,1024]{1,0:T(8,128)(2,1)S(1)}, u32[]{:S(2)}, u32[]{:S(2)}) collective-permute-start(bf16[256,1024]{1,0:T(8,128)(2,1)S(1)} %constant_dynamic-slice_fusion.4), channel_id=1, source_target_pairs={{0,4},{4,0},{1,5},{5,1},{2,6},{6,2},{3,7},{7,3},{8,12},{12,8},{9,1... | collective-permute-start | bytes 1572872 | tf_op jit(solution)/shard_map/ppermute | solution.py:794
  766.3 27.4 %collective-permute-start.4 = (bf16[256,2304]{1,0:T(8,128)(2,1)S(1)}, bf16[256,2304]{1,0:T(8,128)(2,1)S(1)}, u32[]{:S(2)}, u32[]{:S(2)}) collective-permute-start(bf16[256,2304]{1,0:T(8,128)(2,1)S(1)} %constant_dynamic-slice_fusion.3), channel_id=1, source_target_pairs={{0,4},{4,0},{1,5},{5,1},{2,6},{6,2},{3,7},{7,3},{8,12},{12,8},{9,1... | collective-permute-start | bytes 3538952 | tf_op jit(solution)/shard_map/ppermute | solution.py:794
  768.2 25.5 %copy-start.3 = (bf16[512,2304]{1,0:T(8,128)(2,1)S(1)}, bf16[512,2304]{1,0:T(8,128)(2,1)}, u32[]{:S(2)}) copy-start(bf16[512,2304]{1,0:T(8,128)(2,1)} %reduce-scatter.6.cloned.1.call-done) | copy-start | bytes 7077892
Sparse Core Ops, SparseCore 0:
  11.0 48.3 all-gather.4
  61.0 44.4 all-gather.6
  107.0 165.5 all-gather.8
  274.0 61.6 all-gather.10
  369.7 57.5 reduce-scatter.7
  522.7 73.9 reduce-scatter.3
  599.1 165.8 reduce-scatter.5
